TPU v7x, 32 devices: a whole 2x2x4 slice. The times are simulated.
32 devices in a mesh: dp: 8 (over y, x, core), tensor: 4 (over z).
Axes of the slice: x: 2, y: 2, z: 4, core: 2. Of those that a mesh axis runs over, the one named last changes fastest.
Arguments:
- layer_input: float32 [2048, 768], P(('dp', 'tensor')), may hold values from -6 to 6
- segments: int32 [8, 256], P('dp'), may hold values from 0 to 2, as said below
- routes: int32 [2048, 2], P('dp'), may hold values from 0 to 15, all different within a row; in each aligned block of 256 rows (0 to 255, 256 to 511, ...) at most 48 rows name the same one
- gate_weights: float32 [2048, 2], P('dp'), may hold values from 0.2 to 1
- first_gain: bfloat16 [768], P(('dp', 'tensor')), may hold values from 0.5 to 1.5
- first_query: bfloat16 [768, 768], P('dp', 'tensor'), may hold values from -0.21875 to 0.21875
- first_key: bfloat16 [768, 768], P('dp', 'tensor'), may hold values from -0.21875 to 0.21875
- first_value: bfloat16 [768, 768], P('dp', 'tensor'), may hold values from -0.21875 to 0.21875
- first_output: bfloat16 [768, 768], P('tensor', 'dp'), may hold values from -0.875 to 0.875
- first_bias: bfloat16 [32, 12], P('dp', 'tensor'), may hold values from -2 to 300
- first_dense_gain: bfloat16 [768], P(('dp', 'tensor')), may hold values from 0.5 to 1.5
- first_dense_up: bfloat16 [768, 3072], P('dp', 'tensor'), may hold values from -0.21875 to 0.21875
- first_dense_down: bfloat16 [3072, 768], P('tensor', 'dp'), may hold values from -0.109375 to 0.109375
- second_gain: bfloat16 [768], P(('dp', 'tensor')), may hold values from 0.5 to 1.5
- second_query: bfloat16 [768, 768], P('dp', 'tensor'), may hold values from -0.21875 to 0.21875
- second_key: bfloat16 [768, 768], P('dp', 'tensor'), may hold values from -0.21875 to 0.21875
- second_value: bfloat16 [768, 768], P('dp', 'tensor'), may hold values from -0.21875 to 0.21875
- second_output: bfloat16 [768, 768], P('tensor', 'dp'), may hold values from -0.875 to 0.875
- second_bias: bfloat16 [32, 12], P('dp', 'tensor'), may hold values from -2 to 300
- second_expert_gain: bfloat16 [768], P(('dp', 'tensor')), may hold values from 0.5 to 1.5
- expert_up: bfloat16 [16, 768, 3072], P('dp', None, 'tensor'), may hold values from -0.21875 to 0.21875
- expert_down: bfloat16 [16, 3072, 768], P('dp', 'tensor'), may hold values from -0.109375 to 0.109375
- output_grad: float32 [2048, 768], P(('dp', 'tensor')), may hold values from -6 to 6
Outputs:
- layer_output: float32 [2048, 768], P(('dp', 'tensor'))
- input_grad: float32 [2048, 768], P(('dp', 'tensor'))
- first_gain_grad: float32 [768], P(('dp', 'tensor'))
- first_query_grad: float32 [768, 768], P('dp', 'tensor')
- first_key_grad: float32 [768, 768], P('dp', 'tensor')
- first_value_grad: float32 [768, 768], P('dp', 'tensor')
- first_output_grad: float32 [768, 768], P('tensor', 'dp')
- first_bias_grad: float32 [32, 12], P('dp', 'tensor')
- first_dense_gain_grad: float32 [768], P(('dp', 'tensor'))
- first_dense_up_grad: float32 [768, 3072], P('dp', 'tensor')
- first_dense_down_grad: float32 [3072, 768], P('tensor', 'dp')
- second_gain_grad: float32 [768], P(('dp', 'tensor'))
- second_query_grad: float32 [768, 768], P('dp', 'tensor')
- second_key_grad: float32 [768, 768], P('dp', 'tensor')
- second_value_grad: float32 [768, 768], P('dp', 'tensor')
- second_output_grad: float32 [768, 768], P('tensor', 'dp')
- second_bias_grad: float32 [32, 12], P('dp', 'tensor')
- second_expert_gain_grad: float32 [768], P(('dp', 'tensor'))
- expert_up_grad: float32 [16, 768, 3072], P('dp', None, 'tensor')
- expert_down_grad: float32 [16, 3072, 768], P('dp', 'tensor')
Inputs may be any that keep to these rules, and one draw needn't show every extreme that they name: `segments`: documents of at most 2000 tokens, and at least 200 except where cut, are laid end to end over all sequences in order, so a sequence's first and last documents may be cut short. Within a sequence segment numbers start at 0 and never fall. `routes`: each token names 2 different experts. Within one sequence's 256 tokens no expert is named more than 48 times, a bound that some block reaches.
All inputs are finite; a program needn't handle non-finite values.
Results may differ from a plain program's by a relative error of at most 0.024.
Values may be sent and summed in bfloat16 or wider, within the bound.
A program may use at most 128 MiB of HBM per device.

v0:
```python
import math

import jax
import jax.numpy as jnp
import numpy as np
from jax import lax
from jax.sharding import PartitionSpec as P

DH = 64
BUCKETS = 32


EPSILON = 1e-06
NEG_FILL = -1e30
HALF_ROOT = 0.7071067811865476
BELL_SCALE = 0.3989422804014327


def bucket_onehot(length, buckets):
    exact_count = buckets // 2
    distance = np.arange(length)
    result = np.minimum(distance, exact_count)
    for bucket_level in range(1, exact_count):
        threshold = int(
            np.ceil(exact_count * (128.0 / exact_count) ** (bucket_level / exact_count))
        )
        result = result + (distance >= threshold)
    return (result[:, None] == np.arange(buckets)[None, :]).astype(np.float32)


def gelu_value(inputs):
    return 0.5 * inputs * (1.0 + lax.erf(inputs * HALF_ROOT))


def gelu_slope(inputs):
    return (
        0.5 * (1.0 + lax.erf(inputs * HALF_ROOT))
        + inputs * jnp.exp(-0.5 * inputs * inputs) * BELL_SCALE
    )


def norm_rows(token_rows, gain_full):
    values = token_rows.astype(jnp.float32)
    inv_rms = lax.rsqrt(jnp.mean(values * values, axis=-1, keepdims=True) + EPSILON)
    normal = values * inv_rms
    return ((normal * gain_full).astype(jnp.bfloat16), normal, inv_rms)


def norm_back(grad_normed, normal, inv_rms, gain_full):
    grad_normal = grad_normed * gain_full
    grad_part = inv_rms * (
        grad_normal - normal * jnp.mean(grad_normal * normal, axis=-1, keepdims=True)
    )
    return (grad_part, jnp.sum(grad_normed * normal, axis=0))


def gain_from_pieces(pieces, layout):
    dp_count, tensor_count = layout
    piece_width = pieces.shape[0] // (dp_count * tensor_count)
    return pieces.reshape(tensor_count, dp_count, piece_width).transpose(1, 0, 2).reshape(-1)


def gain_to_pieces(full_grad, layout):
    dp_count, tensor_count = layout
    piece_width = full_grad.shape[0] // (dp_count * tensor_count)
    return full_grad.reshape(dp_count, tensor_count, piece_width).transpose(1, 0, 2).reshape(-1)


def fetch_block(query_w, key_w, value_w, output_w, bias_w, gain_attn, gain_mix):
    return (
        lax.all_gather(query_w, "dp", axis=0, tiled=True),
        lax.all_gather(key_w, "dp", axis=0, tiled=True),
        lax.all_gather(value_w, "dp", axis=0, tiled=True),
        lax.all_gather(output_w, "dp", axis=1, tiled=True),
        lax.all_gather(bias_w, "dp", axis=0, tiled=True),
        lax.all_gather(gain_attn, "dp", axis=0, tiled=True),
        lax.all_gather(gain_mix, "dp", axis=0, tiled=True),
    )


def send_block_grads(query_g, key_g, value_g, output_g, bias_g, attn_piece, mix_piece):
    return (
        lax.psum_scatter(query_g, "dp", scatter_dimension=0, tiled=True),
        lax.psum_scatter(key_g, "dp", scatter_dimension=0, tiled=True),
        lax.psum_scatter(value_g, "dp", scatter_dimension=0, tiled=True),
        lax.psum_scatter(output_g, "dp", scatter_dimension=1, tiled=True),
        lax.psum_scatter(bias_g, "dp", scatter_dimension=0, tiled=True),
        lax.psum_scatter(attn_piece, "dp", scatter_dimension=0, tiled=True),
        lax.psum_scatter(mix_piece, "dp", scatter_dimension=0, tiled=True),
    )


def spread_rows(hidden, gain_part, layout):
    token_rows, gain_pieces = (
        lax.all_gather(hidden.astype(jnp.bfloat16), "tensor", axis=0, tiled=True),
        lax.all_gather(gain_part, "tensor", axis=0, tiled=True),
    )
    gain_full = gain_from_pieces(gain_pieces, layout).astype(jnp.float32)
    normed, normal, inv_rms = norm_rows(token_rows, gain_full)
    return (normed, normal, inv_rms, gain_full)


def spread_grad(cotangent):
    return lax.all_gather(cotangent.astype(jnp.bfloat16), "tensor", axis=0, tiled=True)


def collect_rows(partial_out):
    return lax.psum_scatter(partial_out, "tensor", scatter_dimension=0, tiled=True)


def reduce_back(cotangent, grad_normed, normal, inv_rms, gain_full, layout):
    grad_part, gain_grad = norm_back(grad_normed, normal, inv_rms, gain_full)
    token_rows, gain_piece = (
        lax.psum_scatter(grad_part, "tensor", scatter_dimension=0, tiled=True),
        lax.psum_scatter(
            gain_to_pieces(gain_grad, layout), "tensor", scatter_dimension=0, tiled=True
        ),
    )
    return (cotangent + token_rows, gain_piece)


def diagonal_fill(window, rows_count, cols_count):
    head_count = window.shape[0]
    padded = jnp.pad(window, ((0, 0), (0, 1)))
    tiled_rows = jnp.tile(padded, (1, rows_count))
    start_col = rows_count - 1
    band_rows = tiled_rows[:, start_col : start_col + rows_count * (cols_count + rows_count - 1)]
    return band_rows.reshape(head_count, rows_count, cols_count + rows_count - 1)[:, :, :cols_count]


def block_bias(distance_bias, first_row, block_rows):
    head_count, length = distance_bias.shape
    reversed_bias = jnp.concatenate(
        [distance_bias[:, ::-1], jnp.zeros((head_count, length), jnp.float32)], axis=1
    )
    window = lax.dynamic_slice_in_dim(
        reversed_bias, length - block_rows - first_row, length + block_rows - 1, axis=1
    )
    return diagonal_fill(window, block_rows, length)


def block_scores(queries, key_rows, distance_bias, seg_ids, first_row, block_rows):
    length = key_rows.shape[0]
    scores = jnp.einsum(
        "qhd,khd->hqk", queries, key_rows, preferred_element_type=jnp.float32
    ) / math.sqrt(queries.shape[2])
    scores = scores + block_bias(distance_bias, first_row, block_rows)
    row_positions = first_row + jnp.arange(block_rows, dtype=jnp.int32)
    allowed = (row_positions[:, None] >= jnp.arange(length, dtype=jnp.int32)[None, :]) & (
        seg_ids[:, None] == seg_ids[None, :]
    )
    return jnp.where(allowed[None, :, :], scores, NEG_FILL)


def attend_forward(query_rows, key_rows, value_rows, distance_bias, seg_ids):
    length, head_count, head_width = query_rows.shape
    block_rows = min(length, 512)

    def one_block(block_index):
        first_row = block_index * block_rows
        scores = block_scores(query_rows, key_rows, distance_bias, seg_ids, first_row, block_rows)
        highest = jnp.max(scores, axis=-1, keepdims=True)
        exp_scores = jnp.exp(scores - highest)
        row_total = jnp.sum(exp_scores, axis=-1, keepdims=True)
        shares = (exp_scores / row_total).astype(jnp.bfloat16)
        mixed_rows = jnp.einsum(
            "hqk,khd->qhd", shares, value_rows, preferred_element_type=jnp.float32
        ).astype(jnp.bfloat16)
        return (mixed_rows, highest[:, :, 0] + jnp.log(row_total[:, :, 0]))

    mixed_rows, log_total = lax.map(one_block, jnp.arange(length // block_rows, dtype=jnp.int32))
    return (mixed_rows.reshape(length, head_count, head_width), log_total)


def attend_backward(
    query_rows, key_rows, value_rows, distance_bias, seg_ids, mixed_rows, log_total, grad_mixed
):
    length, head_count, head_width = query_rows.shape
    block_rows = min(length, 512)
    inv_root = 1.0 / math.sqrt(head_width)

    def one_block(running, block_index):
        grad_keys, grad_values, grad_distance = running
        first_row = block_index * block_rows
        scores = block_scores(query_rows, key_rows, distance_bias, seg_ids, first_row, block_rows)
        shares = jnp.exp(scores - log_total[block_index][:, :, None])
        grad_values = grad_values + jnp.einsum(
            "hqk,qhd->khd",
            shares.astype(jnp.bfloat16),
            grad_mixed,
            preferred_element_type=jnp.float32,
        )
        share_grad = jnp.einsum(
            "qhd,khd->hqk", grad_mixed, value_rows, preferred_element_type=jnp.float32
        )
        row_dot = jnp.einsum(
            "qhd,qhd->hq", grad_mixed, mixed_rows, preferred_element_type=jnp.float32
        )
        score_grad = shares * (share_grad - row_dot[:, :, None])

        def bias_of(distance_table):
            return block_bias(distance_table, first_row, block_rows)

        bias_pull = jax.vjp(bias_of, distance_bias)[1]
        grad_distance = grad_distance + bias_pull(score_grad)[0]
        score_low = score_grad.astype(jnp.bfloat16)
        grad_queries = (
            jnp.einsum("hqk,khd->qhd", score_low, key_rows, preferred_element_type=jnp.float32)
            * inv_root
        ).astype(jnp.bfloat16)
        grad_keys = grad_keys + jnp.einsum(
            "hqk,qhd->khd", score_low, query_rows, preferred_element_type=jnp.float32
        )
        return ((grad_keys, grad_values, grad_distance), grad_queries)

    zero_rows = jnp.zeros((length, head_count, head_width), jnp.float32)
    start_state = (zero_rows, zero_rows, jnp.zeros_like(distance_bias))
    final_state, grad_queries = lax.scan(
        one_block, start_state, jnp.arange(length // block_rows, dtype=jnp.int32)
    )
    grad_keys, grad_values, grad_distance = final_state
    return (
        grad_queries.reshape(length, head_count, head_width),
        (grad_keys * inv_root).astype(jnp.bfloat16),
        grad_values.astype(jnp.bfloat16),
        grad_distance,
    )


def attention_forward(hidden, block_set, seg_ids, bucket_table, layout):
    query_w, key_w, value_w, output_w, bias_w, gain_attn, gain_mix = block_set
    normed, normal, inv_rms, gain_full = spread_rows(hidden, gain_attn, layout)
    length = normed.shape[0]
    head_count = query_w.shape[1] // DH
    query_rows = (
        jnp.dot(normed, query_w, preferred_element_type=jnp.float32)
        .astype(jnp.bfloat16)
        .reshape(length, head_count, DH)
    )
    key_rows = (
        jnp.dot(normed, key_w, preferred_element_type=jnp.float32)
        .astype(jnp.bfloat16)
        .reshape(length, head_count, DH)
    )
    value_rows = (
        jnp.dot(normed, value_w, preferred_element_type=jnp.float32)
        .astype(jnp.bfloat16)
        .reshape(length, head_count, DH)
    )
    distance_bias = jnp.dot(
        bucket_table, bias_w.astype(jnp.float32), precision=lax.Precision.HIGHEST
    ).T
    mixed_rows, log_total = attend_forward(query_rows, key_rows, value_rows, distance_bias, seg_ids)
    partial_out = jnp.dot(
        mixed_rows.reshape(length, head_count * DH), output_w, preferred_element_type=jnp.float32
    )
    output = hidden + collect_rows(partial_out)
    return (
        output,
        (
            normed,
            normal,
            inv_rms,
            gain_full,
            query_rows,
            key_rows,
            value_rows,
            mixed_rows,
            log_total,
            distance_bias,
        ),
    )


def attention_backward(cotangent, saved, block_set, seg_ids, bucket_table, layout):
    query_w, key_w, value_w, output_w = (block_set[0], block_set[1], block_set[2], block_set[3])
    (
        normed,
        normal,
        inv_rms,
        gain_full,
        query_rows,
        key_rows,
        value_rows,
        mixed_rows,
        log_total,
        distance_bias,
    ) = saved
    length, head_count, head_width = query_rows.shape
    flat_shape = (length, head_count * head_width)
    grad_rows = spread_grad(cotangent)
    output_grad_w = jnp.dot(
        mixed_rows.reshape(flat_shape).T, grad_rows, preferred_element_type=jnp.float32
    )
    grad_mixed = (
        jnp.dot(grad_rows, output_w.T, preferred_element_type=jnp.float32)
        .astype(jnp.bfloat16)
        .reshape(length, head_count, head_width)
    )
    grad_queries, grad_keys, grad_values, grad_distance = attend_backward(
        query_rows, key_rows, value_rows, distance_bias, seg_ids, mixed_rows, log_total, grad_mixed
    )
    bias_grad = jnp.dot(bucket_table.T, grad_distance.T, precision=lax.Precision.HIGHEST)
    grad_queries = grad_queries.reshape(flat_shape)
    grad_keys = grad_keys.reshape(flat_shape)
    grad_values = grad_values.reshape(flat_shape)
    query_grad = jnp.dot(normed.T, grad_queries, preferred_element_type=jnp.float32)
    key_grad = jnp.dot(normed.T, grad_keys, preferred_element_type=jnp.float32)
    value_grad = jnp.dot(normed.T, grad_values, preferred_element_type=jnp.float32)
    grad_normed = jnp.dot(grad_queries, query_w.T, preferred_element_type=jnp.float32)
    grad_normed = grad_normed + jnp.dot(grad_keys, key_w.T, preferred_element_type=jnp.float32)
    grad_normed = grad_normed + jnp.dot(grad_values, value_w.T, preferred_element_type=jnp.float32)
    new_grad, gain_piece = reduce_back(cotangent, grad_normed, normal, inv_rms, gain_full, layout)
    return (new_grad, gain_piece, (query_grad, key_grad, value_grad, output_grad_w, bias_grad))


def dense_forward(hidden, gain_part, dense_up, dense_down, layout):
    normed, normal, inv_rms, gain_full = spread_rows(hidden, gain_part, layout)
    pre_act = jnp.dot(normed, dense_up, preferred_element_type=jnp.float32)
    active = gelu_value(pre_act).astype(jnp.bfloat16)
    output = hidden + collect_rows(jnp.dot(active, dense_down, preferred_element_type=jnp.float32))
    return (output, (normed, normal, inv_rms, gain_full, pre_act, active))


def dense_backward(cotangent, saved, dense_up, dense_down, layout):
    normed, normal, inv_rms, gain_full, pre_act, active = saved
    grad_rows = spread_grad(cotangent)
    down_grad = jnp.dot(active.T, grad_rows, preferred_element_type=jnp.float32)
    grad_pre = (
        jnp.dot(grad_rows, dense_down.T, preferred_element_type=jnp.float32) * gelu_slope(pre_act)
    ).astype(jnp.bfloat16)
    up_grad = jnp.dot(normed.T, grad_pre, preferred_element_type=jnp.float32)
    grad_normed = jnp.dot(grad_pre, dense_up.T, preferred_element_type=jnp.float32)
    up_part, down_part = (
        lax.psum_scatter(up_grad, "dp", scatter_dimension=0, tiled=True),
        lax.psum_scatter(down_grad, "dp", scatter_dimension=1, tiled=True),
    )
    new_grad, gain_piece = reduce_back(cotangent, grad_normed, normal, inv_rms, gain_full, layout)
    return (new_grad, gain_piece, up_part, down_part)


def slot_plan(routes, expert_count, capacity):
    length, top_count = routes.shape
    flat_routes = routes.reshape(-1)
    onehot = (flat_routes[:, None] == jnp.arange(expert_count, dtype=jnp.int32)[None, :]).astype(
        jnp.int32
    )
    before = jnp.cumsum(onehot, axis=0) - onehot
    slot_ids = flat_routes * capacity + jnp.sum(onehot * before, axis=1)
    slot_owner = (
        jnp.full((expert_count * capacity,), length * top_count, jnp.int32)
        .at[slot_ids]
        .set(jnp.arange(length * top_count, dtype=jnp.int32))
    )
    return (slot_ids.reshape(length, top_count), slot_owner)


def expert_forward(hidden, gain_part, routes, gate_weights, expert_up, expert_down, layout):
    dp_count, tensor_count = layout
    normed, normal, inv_rms, gain_full = spread_rows(hidden, gain_part, layout)
    length, top_count = routes.shape
    feature_count = normed.shape[1]
    local_experts = expert_up.shape[0]
    expert_count = local_experts * dp_count
    capacity = max(2, 3 * length * top_count // (2 * expert_count))
    slot_ids, slot_owner = slot_plan(routes, expert_count, capacity)
    padded = jnp.concatenate([normed, jnp.zeros((1, feature_count), jnp.bfloat16)], axis=0)
    sent_rows = padded[slot_owner // top_count].reshape(
        dp_count, local_experts, capacity, feature_count
    )
    arrived = lax.all_to_all(sent_rows, "dp", split_axis=0, concat_axis=0, tiled=True)
    pre_act = jnp.einsum("secd,edf->secf", arrived, expert_up, preferred_element_type=jnp.float32)
    active = gelu_value(pre_act).astype(jnp.bfloat16)
    expert_rows = jnp.einsum(
        "secf,efd->secd", active, expert_down, preferred_element_type=jnp.float32
    )
    returned = lax.all_to_all(expert_rows, "dp", split_axis=0, concat_axis=0, tiled=True)
    picked = returned.reshape(-1, returned.shape[3])[slot_ids]
    combined = jnp.sum(picked * gate_weights[:, :, None], axis=1)
    expert_out = collect_rows(combined)
    return (
        hidden + expert_out,
        (normal, inv_rms, gain_full, slot_ids, slot_owner, arrived, pre_act, active),
    )


def expert_backward(cotangent, saved, gate_weights, expert_up, expert_down, layout):
    normal, inv_rms, gain_full, slot_ids, slot_owner, arrived, pre_act, active = saved
    grad_rows = spread_grad(cotangent)
    length, top_count = gate_weights.shape
    feature_count = grad_rows.shape[1]
    scaled = (gate_weights[:, :, None] * grad_rows.astype(jnp.float32)[:, None, :]).astype(
        jnp.bfloat16
    )
    padded = jnp.concatenate(
        [
            scaled.reshape(length * top_count, feature_count),
            jnp.zeros((1, feature_count), jnp.bfloat16),
        ],
        axis=0,
    )
    sent_grad = padded[slot_owner].reshape(arrived.shape)
    arrived_grad = lax.all_to_all(sent_grad, "dp", split_axis=0, concat_axis=0, tiled=True)
    grad_active = jnp.einsum(
        "secd,efd->secf", arrived_grad, expert_down, preferred_element_type=jnp.float32
    )
    grad_pre = (grad_active * gelu_slope(pre_act)).astype(jnp.bfloat16)
    down_grad = jnp.einsum(
        "secf,secd->efd", active, arrived_grad, preferred_element_type=jnp.float32
    )
    up_grad = jnp.einsum("secd,secf->edf", arrived, grad_pre, preferred_element_type=jnp.float32)
    grad_sent = jnp.einsum(
        "secf,edf->secd", grad_pre, expert_up, preferred_element_type=jnp.float32
    )
    grad_back = lax.all_to_all(grad_sent, "dp", split_axis=0, concat_axis=0, tiled=True)
    grad_normed = jnp.sum(grad_back.reshape(-1, grad_back.shape[3])[slot_ids], axis=1)
    new_grad, gain_piece = reduce_back(cotangent, grad_normed, normal, inv_rms, gain_full, layout)
    return (new_grad, gain_piece, up_grad, down_grad)


def on_device(
    layer_input,
    segments,
    routes,
    gate_weights,
    first_gain,
    first_query,
    first_key,
    first_value,
    first_output,
    first_bias,
    first_dense_gain,
    first_dense_up,
    first_dense_down,
    second_gain,
    second_query,
    second_key,
    second_value,
    second_output,
    second_bias,
    second_expert_gain,
    expert_up,
    expert_down,
    output_grad,
):
    layout = (lax.axis_size("dp"), lax.axis_size("tensor"))
    seg_ids = segments[0]
    bucket_table = jnp.asarray(bucket_onehot(seg_ids.shape[0], BUCKETS))
    weights_one = fetch_block(
        first_query, first_key, first_value, first_output, first_bias, first_gain, first_dense_gain
    )
    hidden_one, saved_one = attention_forward(
        layer_input, weights_one, seg_ids, bucket_table, layout
    )
    dense_up, dense_down = (
        lax.all_gather(first_dense_up, "dp", axis=0, tiled=True),
        lax.all_gather(first_dense_down, "dp", axis=1, tiled=True),
    )
    hidden_two, saved_two = dense_forward(hidden_one, weights_one[6], dense_up, dense_down, layout)
    weights_two = fetch_block(
        second_query,
        second_key,
        second_value,
        second_output,
        second_bias,
        second_gain,
        second_expert_gain,
    )
    hidden_three, saved_three = attention_forward(
        hidden_two, weights_two, seg_ids, bucket_table, layout
    )
    layer_output, saved_four = expert_forward(
        hidden_three, weights_two[6], routes, gate_weights, expert_up, expert_down, layout
    )
    grad_three, expert_piece, expert_up_grad, expert_down_grad = expert_backward(
        output_grad, saved_four, gate_weights, expert_up, expert_down, layout
    )
    grad_two, attn_piece_two, grads_two = attention_backward(
        grad_three, saved_three, weights_two, seg_ids, bucket_table, layout
    )
    summed_two = send_block_grads(
        grads_two[0],
        grads_two[1],
        grads_two[2],
        grads_two[3],
        grads_two[4],
        attn_piece_two,
        expert_piece,
    )
    grad_one, dense_piece, dense_up_grad, dense_down_grad = dense_backward(
        grad_two, saved_two, dense_up, dense_down, layout
    )
    grad_zero, attn_piece_one, grads_one = attention_backward(
        grad_one, saved_one, weights_one, seg_ids, bucket_table, layout
    )
    summed_one = send_block_grads(
        grads_one[0],
        grads_one[1],
        grads_one[2],
        grads_one[3],
        grads_one[4],
        attn_piece_one,
        dense_piece,
    )
    return (
        layer_output,
        grad_zero,
        summed_one[5],
        summed_one[0],
        summed_one[1],
        summed_one[2],
        summed_one[3],
        summed_one[4],
        summed_one[6],
        dense_up_grad,
        dense_down_grad,
        summed_two[5],
        summed_two[0],
        summed_two[1],
        summed_two[2],
        summed_two[3],
        summed_two[4],
        summed_two[6],
        expert_up_grad,
        expert_down_grad,
    )


def solution(mesh):
    return jax.shard_map(
        on_device,
        mesh=mesh,
        in_specs=(
            P(("dp", "tensor"), None),
            P("dp", None),
            P("dp", None),
            P("dp", None),
            P(("dp", "tensor")),
            P("dp", "tensor"),
            P("dp", "tensor"),
            P("dp", "tensor"),
            P("tensor", "dp"),
            P("dp", "tensor"),
            P(("dp", "tensor")),
            P("dp", "tensor"),
            P("tensor", "dp"),
            P(("dp", "tensor")),
            P("dp", "tensor"),
            P("dp", "tensor"),
            P("dp", "tensor"),
            P("tensor", "dp"),
            P("dp", "tensor"),
            P(("dp", "tensor")),
            P("dp", None, "tensor"),
            P("dp", "tensor", None),
            P(("dp", "tensor"), None),
        ),
        out_specs=(
            P(("dp", "tensor"), None),
            P(("dp", "tensor"), None),
            P(("dp", "tensor")),
            P("dp", "tensor"),
            P("dp", "tensor"),
            P("dp", "tensor"),
            P("tensor", "dp"),
            P("dp", "tensor"),
            P(("dp", "tensor")),
            P("dp", "tensor"),
            P("tensor", "dp"),
            P(("dp", "tensor")),
            P("dp", "tensor"),
            P("dp", "tensor"),
            P("dp", "tensor"),
            P("tensor", "dp"),
            P("dp", "tensor"),
            P(("dp", "tensor")),
            P("dp", None, "tensor"),
            P("dp", "tensor", None),
        ),
        check_vma=False,
    )
```

profile of v0, /device:TPU:0, one launch (start us, length us, event | category | flops | bytes accessed | tf_op | source)
XLA Modules:
  0.0 984.5 jit_solution(4099668044368635250)
XLA Ops:
  8.1 10.7 %all-gather = bf16[8,4,3]{2,1,0:T(4,128)(2,1)S(1)} all-gather(bf16[1,4,3]{2,1,0:T(4,128)(2,1)} %bitcast.291), channel_id=1, replica_groups=mesh['dp'=8,'tensor'=4] {'dp'}, dimensions={0}, use_global_device_ids=true | all-gather | bytes 216 | tf_op jit(solution)/shard_map/all_gather | solution.py:75
  20.1 8.8 all-gather.1
  36.8 13.2 %all-reduce.28 = (bf16[192]{0:T(256)(128)(2,1)S(1)}, bf16[192]{0:T(256)(128)(2,1)S(1)}, bf16[192]{0:T(256)(128)(2,1)S(1)}, bf16[192]{0:T(256)(128)(2,1)S(1)}) all-reduce(bf16[192]{0:T(256)(128)(2,1)S(1)} %dynamic-update-slice, bf16[192]{0:T(256)(128)(2,1)S(1)} %dynamic-update-slice.2, ...), channel_id=1, replica_groups=mesh['dp'=8,'tensor'=4] {'dp'}, use_global_device_ids=true, to_apply=%add.8 | all-reduce | flops 768 | bytes 3072
  50.8 12.7 %all-reduce.29 = (bf16[768]{0:T(1024)(128)(2,1)S(1)}, bf16[768]{0:T(1024)(128)(2,1)}, bf16[768]{0:T(1024)(128)(2,1)}, bf16[768]{0:T(1024)(128)(2,1)}) all-reduce(bf16[768]{0:T(1024)(128)(2,1)S(1)} %dynamic-update-slice.1, bf16[768]{0:T(1024)(128)(2,1)S(1)} %dynamic-update-slice.3, ...), channel_id=1, replica_groups=mesh['dp'=8,'tensor'=4] {'tensor'}, use_global_device_ids=true, to_apply=%add.9 | all-reduce | flops 3072 | bytes 12288
  67.0 14.3 %all_gather.84 = bf16[256,768]{1,0:T(8,128)(2,1)S(1)} all-gather(bf16[64,768]{1,0:T(8,128)(2,1)S(1)} %convert_element_type.249), channel_id=1, replica_groups=mesh['dp'=8,'tensor'=4] {'tensor'}, dimensions={0}, use_global_device_ids=true | all-gather | bytes 491520 | tf_op jit(solution)/shard_map/all_gather | solution.py:95
  81.5 9.7 all_gather.91
  91.3 9.4 all_gather.88
  100.7 8.7 all_gather.89
  111.5 9.6 all_gather.87
  124.6 2.5 slice.54
  127.1 4.5 reshape.366
  139.7 19.6 %reduce-scatter.25.cloned.1.call-done = f32[64,768]{1,0:T(8,128)} async-done(((f32[256,768]{1,0:T(8,128)}), f32[64,768]{1,0:T(8,128)}) %reduce-scatter.25.cloned.1.call-update) | async-done | bytes 196624 | tf_op jit(solution)/shard_map/reduce_scatter | solution.py:108
  160.9 15.2 %all_gather.92 = bf16[256,768]{1,0:T(8,128)(2,1)S(1)} all-gather(bf16[64,768]{1,0:T(8,128)(2,1)S(1)} %get-tuple-element.262), channel_id=1, replica_groups=mesh['dp'=8,'tensor'=4] {'tensor'}, dimensions={0}, use_global_device_ids=true | all-gather | bytes 491520 | tf_op jit(solution)/shard_map/all_gather | solution.py:95
  176.4 2.7 multiply_convert_fusion.1
  179.1 8.7 all-gather.7.cloned.1.call-done
  187.8 2.7 fusion.141
  191.5 2.5 copy.208
  194.0 2.5 slice.56
  196.4 4.5 reshape.370
  203.2 11.0 %all_gather.104 = bf16[192,768]{0,1:T(8,128)(2,1)} all-gather(bf16[192,96]{0,1:T(8,128)(2,1)} %copy.133), channel_id=1, replica_groups=mesh['dp'=8,'tensor'=4] {'dp'}, dimensions={1}, use_global_device_ids=true | all-gather | bytes 331776 | tf_op jit(solution)/shard_map/all_gather | solution.py:74
  214.3 9.5 all_gather.101
  223.7 10.4 %all_gather.102 = bf16[768,192]{1,0:T(8,128)(2,1)} all-gather(bf16[96,192]{1,0:T(8,128)(2,1)} %param.39), channel_id=1, replica_groups=mesh['dp'=8,'tensor'=4] {'dp'}, dimensions={0}, use_global_device_ids=true | all-gather | bytes 331776 | tf_op jit(solution)/shard_map/all_gather | solution.py:72
  234.2 10.4 %all_gather.100 = bf16[768,192]{1,0:T(8,128)(2,1)} all-gather(bf16[96,192]{1,0:T(8,128)(2,1)} %param.40), channel_id=1, replica_groups=mesh['dp'=8,'tensor'=4] {'dp'}, dimensions={0}, use_global_device_ids=true | all-gather | bytes 331776 | tf_op jit(solution)/shard_map/all_gather | solution.py:73
  246.3 14.9 %all_gather.97 = bf16[256,768]{1,0:T(8,128)(2,1)S(1)} all-gather(bf16[64,768]{1,0:T(8,128)(2,1)S(1)} %get-tuple-element.260), channel_id=1, replica_groups=mesh['dp'=8,'tensor'=4] {'tensor'}, dimensions={0}, use_global_device_ids=true | all-gather | bytes 491520 | tf_op jit(solution)/shard_map/all_gather | solution.py:95
  273.2 16.7 %reduce-scatter.29.cloned.1.call-done = f32[64,768]{1,0:T(8,128)} async-done(((f32[256,768]{1,0:T(8,128)}), f32[64,768]{1,0:T(8,128)}) %reduce-scatter.29.cloned.1.call-update) | async-done | bytes 196624 | tf_op jit(solution)/shard_map/reduce_scatter | solution.py:108
  291.5 15.2 %all_gather.105 = bf16[256,768]{1,0:T(8,128)(2,1)S(1)} all-gather(bf16[64,768]{1,0:T(8,128)(2,1)S(1)} %get-tuple-element.258), channel_id=1, replica_groups=mesh['dp'=8,'tensor'=4] {'tensor'}, dimensions={0}, use_global_device_ids=true | all-gather | bytes 491520 | tf_op jit(solution)/shard_map/all_gather | solution.py:95
  308.3 3.6 gather_fusion
  311.8 4.4 all-to-all-start
  317.2 15.0 %all_gather.108 = bf16[256,768]{1,0:T(8,128)(2,1)S(1)} all-gather(bf16[64,768]{1,0:T(8,128)(2,1)S(1)} %convert_element_type.293), channel_id=1, replica_groups=mesh['dp'=8,'tensor'=4] {'tensor'}, dimensions={0}, use_global_device_ids=true | all-gather | bytes 491520 | tf_op jit(solution)/shard_map/all_gather | solution.py:104
  333.8 3.1 mul.363
  339.2 3.6 gather_fusion.2
  342.8 4.4 all-to-all-start.2
  347.2 4.3 fusion.15
  351.5 12.5 %all-to-all-done.2 = bf16[8,2,48,768]{3,2,1,0:T(8,128)(2,1)} async-done(((bf16[8,2,48,768]{3,2,1,0:T(8,128)(2,1)}), bf16[8,2,48,768]{3,2,1,0:T(8,128)(2,1)}, u32[]{:S(2)}, u32[]{:S(2)}) %all-to-all-start.2) | async-done | bytes 1179680 | tf_op jit(solution)/shard_map/all_to_all | solution.py:403
  364.0 4.2 fusion.5
  370.9 3.7 all-to-all-start.3
  374.9 29.1 %all-to-all-done.3 = f32[8,2,48,768]{3,2,1,0:T(8,128)S(1)} async-done(((f32[8,2,48,768]{3,2,1,0:T(8,128)}), f32[8,2,48,768]{3,2,1,0:T(8,128)S(1)}, u32[]{:S(2)}, u32[]{:S(2)}) %all-to-all-start.3) | async-done | bytes 2359328 | tf_op jit(solution)/shard_map/all_to_all | solution.py:415
  404.0 2.6 gather_fusion.3
  412.9 20.6 %reduce-scatter.33.cloned.1.call-done = f32[64,768]{1,0:T(8,128)} async-done(((f32[256,768]{1,0:T(8,128)}), f32[64,768]{1,0:T(8,128)}) %reduce-scatter.33.cloned.1.call-update) | async-done | bytes 196624 | tf_op jit(solution)/shard_map/reduce_scatter | solution.py:114
  435.2 15.2 %all_gather.109 = bf16[256,768]{1,0:T(8,128)(2,1)S(1)} all-gather(bf16[64,768]{1,0:T(8,128)(2,1)S(1)} %get-tuple-element.256), channel_id=1, replica_groups=mesh['dp'=8,'tensor'=4] {'tensor'}, dimensions={0}, use_global_device_ids=true | all-gather | bytes 491520 | tf_op jit(solution)/shard_map/all_gather | solution.py:104
  460.4 3.8 all-to-all-start.1
  464.2 14.0 %reduce-scatter.35.cloned.1.call-done = f32[64,768]{1,0:T(8,128)} async-done(((f32[256,768]{1,0:T(8,128)}), f32[64,768]{1,0:T(8,128)}) %reduce-scatter.35.cloned.1.call-update) | async-done | bytes 196624 | tf_op jit(solution)/shard_map/reduce_scatter | solution.py:114
  479.8 15.4 %all_gather.110 = bf16[256,768]{1,0:T(8,128)(2,1)S(1)} all-gather(bf16[64,768]{1,0:T(8,128)(2,1)S(1)} %get-tuple-element.254), channel_id=1, replica_groups=mesh['dp'=8,'tensor'=4] {'tensor'}, dimensions={0}, use_global_device_ids=true | all-gather | bytes 491520 | tf_op jit(solution)/shard_map/all_gather | solution.py:104
  501.3 2.6 gather_fusion.1
  506.2 2.8 multiply_reduce_fusion
  511.1 13.2 %reduce-scatter.37.cloned.1.call-done = f32[64,768]{1,0:T(8,128)} async-done(((f32[256,768]{1,0:T(8,128)}), f32[64,768]{1,0:T(8,128)}) %reduce-scatter.37.cloned.1.call-update) | async-done | bytes 196624 | tf_op jit(solution)/shard_map/reduce_scatter | solution.py:114
  525.9 17.9 %all_gather.111 = bf16[256,768]{1,0:T(8,128)(2,1)S(1)} all-gather(bf16[64,768]{1,0:T(8,128)(2,1)S(1)} %get-tuple-element.252), channel_id=1, replica_groups=mesh['dp'=8,'tensor'=4] {'tensor'}, dimensions={0}, use_global_device_ids=true | all-gather | bytes 491520 | tf_op jit(solution)/shard_map/all_gather | solution.py:104
  572.4 5.0 convolution_bitcast_fusion.1
  577.4 5.0 convolution_bitcast_fusion
  585.3 3.3 reshape.390
  588.7 2.8 pad.47
  596.4 17.0 %all-reduce.27 = (f32[768]{0:T(1024)S(1)}, f32[768]{0:T(1024)S(1)}, f32[768]{0:T(1024)S(1)}, f32[768]{0:T(1024)S(1)}) all-reduce(f32[768]{0:T(1024)S(1)} %reshape.383, f32[768]{0:T(1024)S(1)} %reshape.387, f32[768]{0:T(1024)S(1)} %reshape.389, f32[768]{0:T(1024)S(1)} %reshape.393), channel_id=10, replica_groups=mesh['dp'=8,'tensor'=4] {'tensor'}, use_global_device_ids=true, to_apply=%region_27.28.clone | all-reduce | flops 3072 | bytes 24576
  613.9 3.3 reshape.384
  617.3 2.9 pad.45
  621.0 12.1 %all-reduce.26 = (f32[192]{0:T(256)S(1)}, f32[32,3]{0,1:T(4,128)S(1)}, f32[192]{0:T(256)S(1)}, f32[192]{0:T(256)S(1)}, f32[32,3]{0,1:T(4,128)S(1)}, /*index=5*/f32[192]{0:T(256)S(1)}) all-reduce(f32[192]{0:T(256)S(1)} %dynamic-slice.11, f32[32,3]{0,1:T(4,128)S(1)} %fusion.145, ...), channel_id=11, replica_groups=mesh['dp'=8,'tensor'=4] {'dp'}, use_global_device_ids=true, to_apply=%region_28.29.clone | all-reduce | flops 960 | bytes 7680
  638.6 14.6 %reduce-scatter.39.cloned.1.call-done = f32[64,768]{1,0:T(8,128)} async-done(((f32[256,768]{1,0:T(8,128)}), f32[64,768]{1,0:T(8,128)}) %reduce-scatter.39.cloned.1.call-update) | async-done | bytes 196624 | tf_op jit(solution)/shard_map/reduce_scatter | solution.py:114
  654.9 36.6 %reduce-scatter.55.cloned.1.call-done = f32[96,192]{1,0:T(8,128)} async-done(((f32[768,192]{1,0:T(8,128)}), f32[96,192]{1,0:T(8,128)}) %reduce-scatter.55.cloned.1.call-update) | async-done | bytes 73744 | tf_op jit(solution)/shard_map/reduce_scatter | solution.py:85
  691.5 38.5 %reduce-scatter.53.cloned.1.call-done = f32[96,192]{1,0:T(8,128)} async-done(((f32[768,192]{1,0:T(8,128)}), f32[96,192]{1,0:T(8,128)}) %reduce-scatter.53.cloned.1.call-update) | async-done | bytes 73744 | tf_op jit(solution)/shard_map/reduce_scatter | solution.py:84
  730.0 38.7 %reduce-scatter.51.cloned.1.call-done = f32[96,192]{1,0:T(8,128)} async-done(((f32[768,192]{1,0:T(8,128)}), f32[96,192]{1,0:T(8,128)}) %reduce-scatter.51.cloned.1.call-update) | async-done | bytes 73744 | tf_op jit(solution)/shard_map/reduce_scatter | solution.py:83
  768.7 38.5 %reduce-scatter.45.cloned.1.call-done = f32[96,192]{1,0:T(8,128)} async-done(((f32[768,192]{1,0:T(8,128)}), f32[96,192]{1,0:T(8,128)}) %reduce-scatter.45.cloned.1.call-update) | async-done | bytes 73744 | tf_op jit(solution)/shard_map/reduce_scatter | solution.py:85
  807.2 38.5 %reduce-scatter.43.cloned.1.call-done = f32[96,192]{1,0:T(8,128)} async-done(((f32[768,192]{1,0:T(8,128)}), f32[96,192]{1,0:T(8,128)}) %reduce-scatter.43.cloned.1.call-update) | async-done | bytes 73744 | tf_op jit(solution)/shard_map/reduce_scatter | solution.py:84
  845.8 38.5 %reduce-scatter.41.cloned.1.call-done = f32[96,192]{1,0:T(8,128)} async-done(((f32[768,192]{1,0:T(8,128)}), f32[96,192]{1,0:T(8,128)}) %reduce-scatter.41.cloned.1.call-update) | async-done | bytes 73744 | tf_op jit(solution)/shard_map/reduce_scatter | solution.py:83
  884.3 46.1 %reduce-scatter.47.cloned.1.call-done = f32[96,768]{1,0:T(8,128)} async-done(((f32[768,768]{1,0:T(8,128)}), f32[96,768]{1,0:T(8,128)}) %reduce-scatter.47.cloned.1.call-update) | async-done | bytes 294928 | tf_op jit(solution)/shard_map/reduce_scatter | solution.py:335
  930.4 46.1 %reduce-scatter.49.cloned.1.call-done = f32[768,96]{0,1:T(8,128)} async-done(((f32[768,768]{0,1:T(8,128)}), f32[768,96]{0,1:T(8,128)}) %reduce-scatter.49.cloned.1.call-update) | async-done | bytes 294928 | tf_op jit(solution)/shard_map/reduce_scatter | solution.py:336
  (481 shorter events, 128.8 us)
Async XLA Ops:
  8.0 339.2 %copy-start = (bf16[2,768,768]{2,1,0:T(8,128)(2,1)S(1)}, bf16[2,768,768]{2,1,0:T(8,128)(2,1)}, u32[]{:S(2)}) copy-start(bf16[2,768,768]{2,1,0:T(8,128)(2,1)} %param.44) | copy-start | bytes 7077892
  8.0 83.2 %copy-start.83 = (bf16[96,192]{1,0:T(8,128)(2,1)S(1)}, bf16[96,192]{1,0:T(8,128)(2,1)}, u32[]{:S(2)}) copy-start(bf16[96,192]{1,0:T(8,128)(2,1)} %param.29) | copy-start | bytes 110596
  8.1 151.2 %reduce-scatter.25.cloned.1.call-start = ((), (), s32[]{:S(2)}) async-start(), calls=%async_computation.22 | async-start | bytes 983040 | tf_op jit(solution)/shard_map/reduce_scatter | solution.py:108
  64.6 36.1 %copy-start.84 = (bf16[96,192]{1,0:T(8,128)(2,1)S(1)}, bf16[96,192]{1,0:T(8,128)(2,1)}, u32[]{:S(2)}) copy-start(bf16[96,192]{1,0:T(8,128)(2,1)} %param.30) | copy-start | bytes 110596
  81.5 39.6 %copy-start.94 = (f32[256]{0:T(256)}, f32[256]{0:T(256)S(1)}, u32[]{:S(2)}) copy-start(f32[256]{0:T(256)S(1)} %add_rsqrt_fusion.3) | copy-start | bytes 3076
  81.5 29.9 %copy-start.85 = (bf16[96,192]{1,0:T(8,128)(2,1)S(1)}, bf16[96,192]{1,0:T(8,128)(2,1)}, u32[]{:S(2)}) copy-start(bf16[96,192]{1,0:T(8,128)(2,1)} %param.31) | copy-start | bytes 110596
  100.7 21.5 %copy-start.27 = (bf16[768,192]{1,0:T(8,128)(2,1)}, bf16[768,192]{1,0:T(8,128)(2,1)S(1)}, u32[]{:S(2)}) copy-start(bf16[768,192]{1,0:T(8,128)(2,1)S(1)} %all_gather.88) | copy-start | bytes 884740
  109.4 12.7 %copy-start.109 = (f32[3,256]{1,0:T(4,128)S(1)}, f32[3,256]{1,0:T(4,128)}, u32[]{:S(2)}) copy-start(f32[3,256]{1,0:T(4,128)} %rev.21) | copy-start | bytes 9220
  109.4 12.7 %copy-start.120 = (pred[512]{0:T(512)(128)(4,1)S(1)}, pred[512]{0:T(512)(128)(4,1)}, u32[]{:S(2)}) copy-start(pred[512]{0:T(512)(128)(4,1)} %constant.119.clone.1) | copy-start | bytes 1540
  137.1 22.2 %copy-start.57 = (f32[64,768]{1,0:T(8,128)S(1)}, f32[64,768]{1,0:T(8,128)}, u32[]{:S(2)}) copy-start(f32[64,768]{1,0:T(8,128)} %param.24) | copy-start | bytes 589828
  138.3 38.1 %all-gather.5.cloned.1.call-start = ((), (), s32[]{:S(2)}) async-start(), calls=%async_computation.23 | async-start | bytes 1327104 | tf_op jit(solution)/shard_map/all_gather | solution.py:456
  138.9 48.9 %all-gather.7.cloned.1.call-start = ((), (), s32[]{:S(2)}) async-start(), calls=%async_computation.24 | async-start | bytes 1327104 | tf_op jit(solution)/shard_map/all_gather | solution.py:457
  139.4 105.2 %reduce-scatter.27.cloned.1.call-start = ((), (), s32[]{:S(2)}) async-start(), calls=%async_computation.25 | async-start | bytes 983040 | tf_op jit(solution)/shard_map/reduce_scatter | solution.py:108
  139.7 39.4 %copy-start.87 = (f32[768]{0:T(1024)}, f32[768]{0:T(1024)S(1)}, u32[]{:S(2)}) copy-start(f32[768]{0:T(1024)S(1)} %reshape.395) | copy-start | bytes 9220
  176.3 14.1 %copy-start.111 = (f32[256]{0:T(256)}, f32[256]{0:T(256)S(1)}, u32[]{:S(2)}) copy-start(f32[256]{0:T(256)S(1)} %add_rsqrt_fusion.2) | copy-start | bytes 3076
  179.1 11.4 %copy-start.23 = (bf16[256,768]{1,0:T(8,128)(2,1)}, bf16[256,768]{1,0:T(8,128)(2,1)S(1)}, u32[]{:S(2)}) copy-start(bf16[256,768]{1,0:T(8,128)(2,1)S(1)} %get-tuple-element.276) | copy-start | bytes 1179652
  190.5 99.4 %reduce-scatter.29.cloned.1.call-start = ((), (), s32[]{:S(2)}) async-start(), calls=%async_computation.26 | async-start | bytes 983040 | tf_op jit(solution)/shard_map/reduce_scatter | solution.py:108
  190.8 71.4 %copy-start.76 = (f32[768]{0:T(1024)}, f32[768]{0:T(1024)S(1)}, u32[]{:S(2)}) copy-start(f32[768]{0:T(1024)S(1)} %reshape.396) | copy-start | bytes 9220
  203.2 41.4 %copy-start.65 = (f32[64,768]{1,0:T(8,128)S(1)}, f32[64,768]{1,0:T(8,128)}, u32[]{:S(2)}) copy-start(f32[64,768]{1,0:T(8,128)} %get-tuple-element.263) | copy-start | bytes 589828
  223.7 38.0 %copy-start.28 = (bf16[768,192]{1,0:T(8,128)(2,1)}, bf16[768,192]{1,0:T(8,128)(2,1)S(1)}, u32[]{:S(2)}) copy-start(bf16[768,192]{1,0:T(8,128)(2,1)S(1)} %all_gather.101) | copy-start | bytes 884740
  244.6 16.8 %copy-start.35 = (bf16[768,192]{1,0:T(8,128)(2,1)S(1)}, bf16[768,192]{1,0:T(8,128)(2,1)}, u32[]{:S(2)}) copy-start(bf16[768,192]{1,0:T(8,128)(2,1)} %all_gather.102) | copy-start | bytes 884740
  246.3 15.9 %copy-start.33 = (bf16[768,192]{1,0:T(8,128)(2,1)S(1)}, bf16[768,192]{1,0:T(8,128)(2,1)}, u32[]{:S(2)}) copy-start(bf16[768,192]{1,0:T(8,128)(2,1)} %all_gather.100) | copy-start | bytes 884740
  264.6 25.3 %copy-start.62 = (f32[64,768]{1,0:T(8,128)S(1)}, f32[64,768]{1,0:T(8,128)}, u32[]{:S(2)}) copy-start(f32[64,768]{1,0:T(8,128)} %get-tuple-element.261) | copy-start | bytes 589828
  289.9 18.2 %copy-start.81 = (f32[768]{0:T(1024)S(1)}, f32[768]{0:T(1024)}, u32[]{:S(2)}) copy-start(f32[768]{0:T(1024)} %reshape.397) | copy-start | bytes 9220
  311.8 4.4 copy-start.58
  311.8 4.4 copy-start.116
  311.8 30.9 %all-to-all-start = ((bf16[8,2,48,768]{3,2,1,0:T(8,128)(2,1)}), bf16[8,2,48,768]{3,2,1,0:T(8,128)(2,1)}, u32[]{:S(2)}, u32[]{:S(2)}) async-start(bf16[8,2,48,768]{3,2,1,0:T(8,128)(2,1)} %bitcast.240), calls=%async_computation.3 | async-start | bytes 2359296 | tf_op jit(solution)/shard_map/all_to_all | solution.py:371
  342.8 21.2 %all-to-all-start.2 = ((bf16[8,2,48,768]{3,2,1,0:T(8,128)(2,1)}), bf16[8,2,48,768]{3,2,1,0:T(8,128)(2,1)}, u32[]{:S(2)}, u32[]{:S(2)}) async-start(bf16[8,2,48,768]{3,2,1,0:T(8,128)(2,1)} %bitcast.241), calls=%async_computation.6 | async-start | bytes 2359296 | tf_op jit(solution)/shard_map/all_to_all | solution.py:403
  370.9 33.1 %all-to-all-start.3 = ((f32[8,2,48,768]{3,2,1,0:T(8,128)}), f32[8,2,48,768]{3,2,1,0:T(8,128)S(1)}, u32[]{:S(2)}, u32[]{:S(2)}) async-start(f32[8,2,48,768]{3,2,1,0:T(8,128)} %copy.144), calls=%async_computation.7 | async-start | bytes 4718592 | tf_op jit(solution)/shard_map/all_to_all | solution.py:415
  374.7 58.9 %reduce-scatter.33.cloned.1.call-start = ((), (), s32[]{:S(2)}) async-start(), calls=%async_computation.28 | async-start | bytes 983040 | tf_op jit(solution)/shard_map/reduce_scatter | solution.py:114
  411.7 21.9 %copy-start.59 = (f32[64,768]{1,0:T(8,128)S(1)}, f32[64,768]{1,0:T(8,128)}, u32[]{:S(2)}) copy-start(f32[64,768]{1,0:T(8,128)} %param.46) | copy-start | bytes 589828
  411.7 38.7 %copy-start.17 = (bf16[192,768]{0,1:T(8,128)(2,1)S(1)}, bf16[192,768]{0,1:T(8,128)(2,1)}, u32[]{:S(2)}) copy-start(bf16[192,768]{0,1:T(8,128)(2,1)} %all_gather.104) | copy-start | bytes 884740
  412.8 38.0 %copy-start.52 = (bf16[3,64,256]{2,1,0:T(8,128)(2,1)S(1)}, bf16[3,64,256]{2,1,0:T(8,128)(2,1)}, u32[]{:S(2)}) copy-start(bf16[3,64,256]{2,1,0:T(8,128)(2,1)} %copy-done.51) | copy-start | bytes 294916
  412.8 38.0 %copy-start.9 = (f32[3,256,256]{1,2,0:T(8,128)S(1)}, f32[3,256,256]{1,2,0:T(8,128)}, u32[]{:S(2)}) copy-start(f32[3,256,256]{1,2,0:T(8,128)} %copy-done.8) | copy-start | bytes 2359300
  412.8 65.3 %reduce-scatter.35.cloned.1.call-start = ((), (), s32[]{:S(2)}) async-start(), calls=%async_computation.29 | async-start | bytes 983040 | tf_op jit(solution)/shard_map/reduce_scatter | solution.py:114
  412.9 38.2 %copy-start.80 = (bf16[256,192]{0,1:T(8,128)(2,1)S(1)}, bf16[256,192]{0,1:T(8,128)(2,1)}, u32[]{:S(2)}) copy-start(bf16[256,192]{0,1:T(8,128)(2,1)} %copy-done.79) | copy-start | bytes 294916
  460.4 17.8 %copy-start.64 = (f32[64,768]{1,0:T(8,128)S(1)}, f32[64,768]{1,0:T(8,128)}, u32[]{:S(2)}) copy-start(f32[64,768]{1,0:T(8,128)} %get-tuple-element.257) | copy-start | bytes 589828
  460.4 41.0 %all-to-all-start.1 = ((f32[8,2,48,768]{3,2,1,0:T(8,128)}), f32[8,2,48,768]{3,2,1,0:T(8,128)S(1)}, u32[]{:S(2)}, u32[]{:S(2)}) async-start(f32[8,2,48,768]{3,2,1,0:T(8,128)} %copy.140), calls=%async_computation.4 | async-start | bytes 4718592 | tf_op jit(solution)/shard_map/all_to_all | solution.py:377
  464.1 60.1 %reduce-scatter.37.cloned.1.call-start = ((), (), s32[]{:S(2)}) async-start(), calls=%async_computation.30 | async-start | bytes 983040 | tf_op jit(solution)/shard_map/reduce_scatter | solution.py:114
  501.3 90.8 %reduce-scatter.31.cloned.1.call-start = ((), (), s32[]{:S(2)}) async-start(), calls=%async_computation.27 | async-start | bytes 983040 | tf_op jit(solution)/shard_map/reduce_scatter | solution.py:108
  509.1 15.2 %copy-start.63 = (f32[64,768]{1,0:T(8,128)S(1)}, f32[64,768]{1,0:T(8,128)}, u32[]{:S(2)}) copy-start(f32[64,768]{1,0:T(8,128)} %get-tuple-element.255) | copy-start | bytes 589828
  509.1 85.0 %reduce-scatter.59.cloned.1.call-start = ((), (), s32[]{:S(2)}) async-start(), calls=%async_computation.41 | async-start | bytes 884736
  509.8 34.0 %copy-start.15 = (bf16[192,768]{0,1:T(8,128)(2,1)S(1)}, bf16[192,768]{0,1:T(8,128)(2,1)}, u32[]{:S(2)}) copy-start(bf16[192,768]{0,1:T(8,128)(2,1)} %all_gather.91) | copy-start | bytes 884740
  511.0 33.1 %copy-start.50 = (bf16[3,64,256]{2,1,0:T(8,128)(2,1)S(1)}, bf16[3,64,256]{2,1,0:T(8,128)(2,1)}, u32[]{:S(2)}) copy-start(bf16[3,64,256]{2,1,0:T(8,128)(2,1)} %copy-done.49) | copy-start | bytes 294916
  511.0 33.2 %copy-start.5 = (f32[3,256,256]{1,2,0:T(8,128)S(1)}, f32[3,256,256]{1,2,0:T(8,128)}, u32[]{:S(2)}) copy-start(f32[3,256,256]{1,2,0:T(8,128)} %copy-done.4) | copy-start | bytes 2359300
  511.0 33.2 %copy-start.93 = (f32[3,256]{1,0:T(4,128)S(1)}, f32[3,256]{1,0:T(4,128)}, u32[]{:S(2)}) copy-start(f32[3,256]{1,0:T(4,128)} %log_add_fusion) | copy-start | bytes 9220
  511.0 125.9 %reduce-scatter.57.cloned.1.call-start = ((), (), s32[]{:S(2)}) async-start(), calls=%async_computation.40 | async-start | bytes 884736
  525.9 19.5 %copy-start.69 = (bf16[256,192]{0,1:T(8,128)(2,1)S(1)}, bf16[256,192]{0,1:T(8,128)(2,1)}, u32[]{:S(2)}) copy-start(bf16[256,192]{0,1:T(8,128)(2,1)} %convolution_convert_fusion.10) | copy-start | bytes 294916
  552.0 101.2 %reduce-scatter.39.cloned.1.call-start = ((), (), s32[]{:S(2)}) async-start(), calls=%async_computation.31 | async-start | bytes 983040 | tf_op jit(solution)/shard_map/reduce_scatter | solution.py:114
  556.8 134.6 %reduce-scatter.55.cloned.1.call-start = ((), (), s32[]{:S(2)}) async-start(), calls=%async_computation.39 | async-start | bytes 884736 | tf_op jit(solution)/shard_map/reduce_scatter | solution.py:85
  558.2 171.8 %reduce-scatter.53.cloned.1.call-start = ((), (), s32[]{:S(2)}) async-start(), calls=%async_computation.38 | async-start | bytes 884736 | tf_op jit(solution)/shard_map/reduce_scatter | solution.py:84
  559.6 209.1 %reduce-scatter.51.cloned.1.call-start = ((), (), s32[]{:S(2)}) async-start(), calls=%async_computation.37 | async-start | bytes 884736 | tf_op jit(solution)/shard_map/reduce_scatter | solution.py:83
  561.0 246.3 %reduce-scatter.45.cloned.1.call-start = ((), (), s32[]{:S(2)}) async-start(), calls=%async_computation.34 | async-start | bytes 884736 | tf_op jit(solution)/shard_map/reduce_scatter | solution.py:85
  562.4 283.4 %reduce-scatter.43.cloned.1.call-start = ((), (), s32[]{:S(2)}) async-start(), calls=%async_computation.33 | async-start | bytes 884736 | tf_op jit(solution)/shard_map/reduce_scatter | solution.py:84
  563.8 320.5 %reduce-scatter.41.cloned.1.call-start = ((), (), s32[]{:S(2)}) async-start(), calls=%async_computation.32 | async-start | bytes 884736 | tf_op jit(solution)/shard_map/reduce_scatter | solution.py:83
  565.2 365.2 %reduce-scatter.47.cloned.1.call-start = ((), (), s32[]{:S(2)}) async-start(), calls=%async_computation.35 | async-start | bytes 2654208 | tf_op jit(solution)/shard_map/reduce_scatter | solution.py:335
  567.3 409.3 %reduce-scatter.49.cloned.1.call-start = ((), (), s32[]{:S(2)}) async-start(), calls=%async_computation.36 | async-start | bytes 2654208 | tf_op jit(solution)/shard_map/reduce_scatter | solution.py:336
  572.4 5.0 copy-start.39
  577.4 5.0 copy-start.104
  577.4 5.2 copy-start.7
  591.4 4.4 copy-start.114
  591.9 4.4 copy-start.106
  617.3 359.3 %copy-start.1 = (bf16[2,768,768]{2,1,0:T(8,128)(2,1)S(1)}, bf16[2,768,768]{2,1,0:T(8,128)(2,1)}, u32[]{:S(2)}) copy-start(bf16[2,768,768]{2,1,0:T(8,128)(2,1)} %param.44) | copy-start | bytes 7077892
  620.2 33.1 %copy-start.61 = (f32[64,768]{1,0:T(8,128)S(1)}, f32[64,768]{1,0:T(8,128)}, u32[]{:S(2)}) copy-start(f32[64,768]{1,0:T(8,128)} %get-tuple-element.253) | copy-start | bytes 589828
  (84 other events, 137.6 us)
Sparse Core Ops, SparseCore 0:
  138.4 20.8 reduce-scatter.24
  190.6 23.1 reduce-scatter.26
  265.9 23.9 reduce-scatter.28
  413.0 20.5 reduce-scatter.32
  455.7 22.3 reduce-scatter.34
  501.4 22.8 reduce-scatter.36
  526.5 25.4 reduce-scatter.30
  555.2 34.4 reduce-scatter.58
  592.8 34.9 reduce-scatter.56
  629.9 23.2 reduce-scatter.38
  657.0 34.4 reduce-scatter.54
  695.0 34.9 reduce-scatter.52
  733.7 34.9 reduce-scatter.50
  772.3 34.9 reduce-scatter.44
  810.8 34.9 reduce-scatter.42
  849.3 34.9 reduce-scatter.40
  888.1 42.3 reduce-scatter.46
  934.2 42.3 reduce-scatter.48
Sparse Core Ops, SparseCore 1:
  140.6 21.4 all-gather.4
  163.9 23.8 all-gather.6
where the time goes:
time: 992 us; the launch traced here: 985 us
  waiting for transfers between devices  472 us (48%)
  blocking collectives  277 us (28%)
  local copies, waits for them, and re-layouts  93.8 us (9%)
  matrix products  69.8 us (7%)
  other arithmetic  33.5 us (3%)
  between operations  21.2 us (2%)
  starting transfers between devices  17.4 us (2%)
    reduce_scatter x2, waiting for transfers between devices, send_block_grads(): lax.psum_scatter(query_g, 'dp', scatter_dimension=0, tiled=True)  77.2 us
    reduce_scatter x2, waiting for transfers between devices, send_block_grads(): lax.psum_scatter(key_g, 'dp', scatter_dimension=0, tiled=True)  77.1 us
    reduce_scatter x2, waiting for transfers between devices, send_block_grads(): lax.psum_scatter(value_g, 'dp', scatter_dimension=0, tiled=True)  75.1 us
    all_gather x4, blocking collectives, spread_grad(): lax.all_gather(cotangent.astype(jnp.bfloat16), 'tensor', axis=0, tiled=True)  63.6 us
    reduce_scatter x4, waiting for transfers between devices, reduce_back(): lax.psum_scatter(grad_part, 'tensor', scatter_dimension=0, tiled=True)  62.4 us
    all_gather x4, blocking collectives, spread_rows(): lax.all_gather(hidden.astype(jnp.bfloat16), 'tensor', axis=0, tiled=True)  59.7 us
    unnamed x4, blocking collectives  55 us
    reduce_scatter x1, waiting for transfers between devices, dense_backward(): lax.psum_scatter(down_grad, 'dp', scatter_dimension=1, tiled=True)  46.1 us
  transfers between devices with their start and end apart: 24, of which 17 were waited for; matrix products, arithmetic and copies ran while one was open for 12% of the time, Pallas kernels for 0%

commit v1 on v0

v1 whole, which is shorter than its diff:
```python
import math

import jax
import jax.numpy as jnp
import numpy as np
from jax import lax
from jax.experimental import pallas as pl
from jax.experimental.pallas import tpu as pltpu
from jax.sharding import PartitionSpec as P

DH = 64
BUCKETS = 32
EPSILON = 1e-06
NEG_FILL = -1e30
HALF_ROOT = 0.7071067811865476
BELL_SCALE = 0.3989422804014327
F32 = jnp.float32
BF16 = jnp.bfloat16


def band_onehot(length, buckets):
    exact_count = buckets // 2
    distance = np.arange(length)
    result = np.minimum(distance, exact_count)
    for bucket_level in range(1, exact_count):
        threshold = int(
            np.ceil(exact_count * (128.0 / exact_count) ** (bucket_level / exact_count))
        )
        result = result + (distance >= threshold)
    band = result[(np.arange(8)[:, None] - np.arange(length)[None, :]) % length]
    return (band.reshape(-1)[:, None] == np.arange(buckets)[None, :]).astype(np.float32)


def gelu_value(inputs):
    return 0.5 * inputs * (1.0 + lax.erf(inputs * HALF_ROOT))


def gelu_slope(inputs):
    return (
        0.5 * (1.0 + lax.erf(inputs * HALF_ROOT))
        + inputs * jnp.exp(-0.5 * inputs * inputs) * BELL_SCALE
    )


def norm_rows(token_rows, gain_full):
    values = token_rows.astype(F32)
    inv_rms = lax.rsqrt(jnp.mean(values * values, axis=-1, keepdims=True) + EPSILON)
    normal = values * inv_rms
    return ((normal * gain_full).astype(BF16), normal, inv_rms)


def norm_back(grad_normed, normal, inv_rms, gain_full):
    grad_normal = grad_normed * gain_full
    grad_part = inv_rms * (
        grad_normal - normal * jnp.mean(grad_normal * normal, axis=-1, keepdims=True)
    )
    return (grad_part, jnp.sum(grad_normed * normal, axis=0, keepdims=True))


def mm(left, right, left_dim=1, right_dim=0):
    return lax.dot_general(
        left, right, (((left_dim,), (right_dim,)), ((), ())), preferred_element_type=F32
    )


def allowed_pairs(seg_row, seg_col):
    length = seg_row.shape[1]
    rows = lax.broadcasted_iota(jnp.int32, (length, length), 0)
    cols = lax.broadcasted_iota(jnp.int32, (length, length), 1)
    return (rows >= cols) & (seg_row == seg_col)


def head_shares(query, key, band, allowed):
    length = query.shape[0]
    bias = jnp.concatenate(
        [pltpu.roll(band, 8 * step, 1) if step else band for step in range(length // 8)], axis=0
    )
    scores = mm(query, key, 1, 1) * (1.0 / math.sqrt(DH)) + bias
    scores = jnp.where(allowed, scores, NEG_FILL)
    exp_scores = jnp.exp(scores - jnp.max(scores, axis=-1, keepdims=True))
    return exp_scores / jnp.sum(exp_scores, axis=-1, keepdims=True)


def attn_forward_kernel(x_ref, g_ref, wqkv_ref, wo_ref, band_ref, segr_ref, segc_ref,
                        qkv_ref, o_ref, part_ref):
    normed, _, _ = norm_rows(x_ref[...], g_ref[...])
    qkv = mm(normed, wqkv_ref[...]).astype(BF16)
    qkv_ref[...] = qkv
    width = o_ref.shape[1]
    allowed = allowed_pairs(segr_ref[...], segc_ref[...])
    mixed = []
    for head in range(width // DH):
        lo = head * DH
        shares = head_shares(
            qkv[:, lo : lo + DH],
            qkv[:, width + lo : width + lo + DH],
            band_ref[head * 8 : head * 8 + 8, :],
            allowed,
        ).astype(BF16)
        mixed.append(mm(shares, qkv[:, 2 * width + lo : 2 * width + lo + DH]).astype(BF16))
    mixed = jnp.concatenate(mixed, axis=1)
    o_ref[...] = mixed
    part_ref[...] = mm(mixed, wo_ref[...], 1, 1).astype(BF16)


def attn_backward_kernel(b_ref, x_ref, g_ref, wqkv_ref, wo_ref, band_ref, segr_ref, segc_ref,
                         qkv_ref, o_ref, wg_ref, part_ref, gain_ref, bandg_ref):
    width = o_ref.shape[1]
    normed, normal, inv_rms = norm_rows(x_ref[...], g_ref[...])
    grad_rows = b_ref[...]
    mixed = o_ref[...]
    qkv = qkv_ref[...]
    grad_mixed = mm(grad_rows, wo_ref[...]).astype(BF16)
    allowed = allowed_pairs(segr_ref[...], segc_ref[...])
    length = qkv.shape[0]
    inv_root = 1.0 / math.sqrt(DH)
    grad_q, grad_k, grad_v = [], [], []
    for head in range(width // DH):
        lo = head * DH
        query = qkv[:, lo : lo + DH]
        key = qkv[:, width + lo : width + lo + DH]
        value = qkv[:, 2 * width + lo : 2 * width + lo + DH]
        grad_head = grad_mixed[:, lo : lo + DH]
        mixed_head = mixed[:, lo : lo + DH]
        shares = head_shares(query, key, band_ref[head * 8 : head * 8 + 8, :], allowed)
        grad_v.append(mm(shares.astype(BF16), grad_head, 0, 0).astype(BF16))
        row_dot = jnp.sum(
            grad_head.astype(F32) * mixed_head.astype(F32), axis=-1, keepdims=True
        )
        score_grad = shares * (mm(grad_head, value, 1, 1) - row_dot)
        total = score_grad[0:8, :]
        for step in range(1, length // 8):
            total = total + pltpu.roll(
                score_grad[8 * step : 8 * step + 8, :], length - 8 * step, 1
            )
        bandg_ref[head * 8 : head * 8 + 8, :] = total
        score_low = score_grad.astype(BF16)
        grad_q.append((mm(score_low, key) * inv_root).astype(BF16))
        grad_k.append((mm(score_low, query, 0, 0) * inv_root).astype(BF16))
    grad_qkv = jnp.concatenate(grad_q + grad_k + grad_v, axis=1)
    wg_ref[...] = jnp.concatenate(
        [mm(normed, grad_qkv, 0, 0).astype(BF16), mm(grad_rows, mixed, 0, 0).astype(BF16)], axis=1
    )
    grad_normed = mm(grad_qkv, wqkv_ref[...], 1, 1)
    grad_part, gain_grad = norm_back(grad_normed, normal, inv_rms, g_ref[...])
    part_ref[...] = grad_part.astype(BF16)
    gain_ref[...] = gain_grad


def dense_forward_kernel(x_ref, g_ref, w_ref, pre_ref, part_ref):
    hidden = pre_ref.shape[1]
    normed, _, _ = norm_rows(x_ref[...], g_ref[...])
    pre = mm(normed, w_ref[:, :hidden])
    pre_ref[...] = pre
    part_ref[...] = mm(gelu_value(pre).astype(BF16), w_ref[:, hidden:], 1, 1).astype(BF16)


def dense_backward_kernel(b_ref, x_ref, g_ref, w_ref, pre_ref, up_ref, down_ref, part_ref,
                          gain_ref):
    hidden = pre_ref.shape[1]
    normed, normal, inv_rms = norm_rows(x_ref[...], g_ref[...])
    grad_rows = b_ref[...]
    pre = pre_ref[...]
    active = gelu_value(pre).astype(BF16)
    down_ref[...] = mm(grad_rows, active, 0, 0).astype(BF16)
    grad_pre = (mm(grad_rows, w_ref[:, hidden:]) * gelu_slope(pre)).astype(BF16)
    up_ref[...] = mm(normed, grad_pre, 0, 0).astype(BF16)
    grad_normed = mm(grad_pre, w_ref[:, :hidden], 1, 1)
    grad_part, gain_grad = norm_back(grad_normed, normal, inv_rms, g_ref[...])
    part_ref[...] = grad_part.astype(BF16)
    gain_ref[...] = gain_grad


def call(kernel, outs, *args):
    return pl.pallas_call(
        kernel,
        out_shape=[jax.ShapeDtypeStruct(shape, dtype) for shape, dtype in outs],
        compiler_params=pltpu.CompilerParams(vmem_limit_bytes=40 * 1024 * 1024),
    )(*args)


def gather_rows(hidden):
    return lax.all_gather(hidden.astype(BF16), "tensor", axis=0, tiled=True)


def swap_sum(parts, axis_name, count):
    blocks = parts.astype(BF16).reshape(count, parts.shape[0] // count, parts.shape[1])
    arrived = lax.all_to_all(blocks, axis_name, split_axis=0, concat_axis=0, tiled=True)
    return jnp.sum(arrived.astype(F32), axis=0)


def swap_blocks(blocks):
    return lax.all_to_all(blocks, "dp", split_axis=0, concat_axis=0, tiled=True)


def slot_plan(routes, expert_count, capacity):
    length, top_count = routes.shape
    flat_routes = routes.reshape(-1)
    onehot = (flat_routes[:, None] == jnp.arange(expert_count, dtype=jnp.int32)[None, :]).astype(
        jnp.int32
    )
    before = jnp.cumsum(onehot, axis=0) - onehot
    slot_ids = flat_routes * capacity + jnp.sum(onehot * before, axis=1)
    return slot_ids.reshape(length, top_count)


def on_device(
    layer_input, segments, routes, gate_weights,
    first_gain, first_query, first_key, first_value, first_output, first_bias,
    first_dense_gain, first_dense_up, first_dense_down,
    second_gain, second_query, second_key, second_value, second_output, second_bias,
    second_expert_gain, expert_up, expert_down, output_grad,
):
    dp_count, tensor_count = lax.axis_size("dp"), lax.axis_size("tensor")
    dp_index, tensor_index = lax.axis_index("dp"), lax.axis_index("tensor")
    length = segments.shape[1]
    features = layer_input.shape[1]
    width = first_query.shape[1]
    heads = first_bias.shape[1]
    hidden = first_dense_up.shape[1]
    piece = first_gain.shape[0]
    bias_rows = first_bias.shape[0]
    table = jnp.asarray(band_onehot(length, BUCKETS))

    small = jnp.concatenate(
        [first_gain, first_dense_gain, second_gain, second_expert_gain,
         first_bias.reshape(-1), second_bias.reshape(-1)]
    )
    pad = (-small.shape[0]) % 128
    small = jnp.pad(small, (0, pad))
    smalls = lax.all_gather(small[None], ("dp", "tensor"), axis=0, tiled=True)
    gains = [
        smalls[:, k * piece : (k + 1) * piece].astype(F32).reshape(1, features) for k in range(4)
    ]
    biases = []
    for k in range(2):
        start = 4 * piece + k * bias_rows * heads
        block = smalls[:, start : start + bias_rows * heads].reshape(
            dp_count, tensor_count, bias_rows, heads
        )
        biases.append(
            lax.dynamic_index_in_dim(block, tensor_index, 1, keepdims=False).reshape(
                dp_count * bias_rows, heads
            )
        )
    bands = [
        jnp.dot(table, bias.astype(F32), precision=lax.Precision.HIGHEST).T.reshape(
            heads * 8, length
        )
        for bias in biases
    ]

    def fetch(*parts):
        return lax.all_gather(jnp.concatenate(parts, axis=1), "dp", axis=0, tiled=True)

    weights_one = fetch(first_query, first_key, first_value, first_output.T)
    weights_dense = fetch(first_dense_up, first_dense_down.T)
    weights_two = fetch(second_query, second_key, second_value, second_output.T)
    seg_row = segments
    seg_col = segments.reshape(length, 1)

    def attn_forward(x_rows, gain, weights, band):
        wqkv, wo = weights[:, : 3 * width], weights[:, 3 * width :]
        qkv, mixed, part = call(
            attn_forward_kernel,
            [((length, 3 * width), BF16), ((length, width), BF16), ((length, features), BF16)],
            x_rows, gain, wqkv, wo, band, seg_row, seg_col,
        )
        return part, (x_rows, gain, wqkv, wo, band, qkv, mixed)

    def attn_backward(grad_rows, saved):
        x_rows, gain, wqkv, wo, band, qkv, mixed = saved
        return call(
            attn_backward_kernel,
            [((features, 4 * width), BF16), ((length, features), BF16), ((1, features), F32),
             ((heads * 8, length), F32)],
            grad_rows, x_rows, gain, wqkv, wo, band, seg_row, seg_col, qkv, mixed,
        )

    def collect(part):
        return swap_sum(part, "tensor", tensor_count)

    top_count = routes.shape[1]
    local_experts = expert_up.shape[0]
    expert_count = local_experts * dp_count
    capacity = max(2, 3 * length * top_count // (2 * expert_count))
    slots = expert_count * capacity
    slot_ids = slot_plan(routes, expert_count, capacity)
    slot_flat = slot_ids.T.reshape(1, top_count * length)
    place = (jnp.arange(slots, dtype=jnp.int32)[:, None] == slot_flat).astype(BF16)
    place_rows = place.reshape(slots, top_count, length).sum(axis=1)
    sent_shape = (dp_count, local_experts, capacity, features)

    out_grad_rows = gather_rows(output_grad)
    scaled = (gate_weights.T[:, :, None] * out_grad_rows.astype(F32)[None]).astype(BF16)
    sent_grad = mm(place, scaled.reshape(top_count * length, features)).astype(BF16)
    arrived_grad = swap_blocks(sent_grad.reshape(sent_shape))

    part, saved_one = attn_forward(gather_rows(layer_input), gains[0], weights_one, bands[0])
    hidden_one = layer_input + collect(part)
    rows_one = gather_rows(hidden_one)
    pre_act, part = call(
        dense_forward_kernel,
        [((length, hidden), F32), ((length, features), BF16)],
        rows_one, gains[1], weights_dense,
    )
    hidden_two = hidden_one + collect(part)
    part, saved_three = attn_forward(gather_rows(hidden_two), gains[2], weights_two, bands[1])
    hidden_three = hidden_two + collect(part)
    rows_three = gather_rows(hidden_three)
    normed, normal, inv_rms = norm_rows(rows_three, gains[3])
    arrived = swap_blocks(mm(place_rows, normed).astype(BF16).reshape(sent_shape))
    pre_expert = jnp.einsum("secd,edf->secf", arrived, expert_up, preferred_element_type=F32)

    grad_active = jnp.einsum(
        "secd,efd->secf", arrived_grad, expert_down, preferred_element_type=F32
    )
    grad_pre = (grad_active * gelu_slope(pre_expert)).astype(BF16)
    grad_sent = jnp.einsum(
        "secf,edf->secd", grad_pre, expert_up, preferred_element_type=F32
    ).astype(BF16)
    grad_back = swap_blocks(grad_sent).reshape(slots, features)
    grad_normed = mm(place_rows, grad_back, 0, 0)
    grad_part, expert_gain_grad = norm_back(grad_normed, normal, inv_rms, gains[3])
    grad_three = output_grad + collect(grad_part)

    active = gelu_value(pre_expert).astype(BF16)
    expert_rows = jnp.einsum(
        "secf,efd->secd", active, expert_down, preferred_element_type=F32
    ).astype(BF16)
    returned = swap_blocks(expert_rows).reshape(slots, features)
    picked = mm(place, returned, 0, 0).reshape(top_count, length, features)
    combined = jnp.sum(picked * gate_weights.T[:, :, None], axis=0)
    layer_output = hidden_three + collect(combined)
    expert_down_grad = jnp.einsum("secf,secd->efd", active, arrived_grad, preferred_element_type=F32)
    expert_up_grad = jnp.einsum("secd,secf->edf", arrived, grad_pre, preferred_element_type=F32)

    wg_two, part, gain_two, band_grad_two = attn_backward(gather_rows(grad_three), saved_three)
    summed_two = swap_sum(wg_two, "dp", dp_count)
    grad_two = grad_three + collect(part)
    up_wg, down_wg, part, gain_dense = call(
        dense_backward_kernel,
        [((features, hidden), BF16), ((features, hidden), BF16), ((length, features), BF16),
         ((1, features), F32)],
        gather_rows(grad_two), rows_one, gains[1], weights_dense, pre_act,
    )
    dense_up_grad = swap_sum(up_wg, "dp", dp_count)
    dense_down_grad = swap_sum(down_wg, "dp", dp_count).T
    grad_one = grad_two + collect(part)
    wg_one, part, gain_one, band_grad_one = attn_backward(gather_rows(grad_one), saved_one)
    summed_one = swap_sum(wg_one, "dp", dp_count)
    grad_zero = grad_one + collect(part)

    mine = (jnp.arange(tensor_count) == tensor_index).astype(F32)

    def spread_bias(band_grad):
        grad = jnp.dot(
            table.T, band_grad.reshape(heads, 8 * length).T, precision=lax.Precision.HIGHEST
        )
        return (grad[:, None, :] * mine[None, :, None]).reshape(-1)

    totals = lax.psum(
        jnp.concatenate(
            [gain_one[0], gain_dense[0], gain_two[0], expert_gain_grad[0],
             spread_bias(band_grad_one), spread_bias(band_grad_two)]
        ),
        ("dp", "tensor"),
    )
    own = (dp_index * tensor_count + tensor_index) * piece
    gain_grads = [
        lax.dynamic_slice_in_dim(totals, k * features + own, piece) for k in range(4)
    ]
    bias_grads = [
        lax.dynamic_slice(
            grad, (dp_index * bias_rows, tensor_index * heads), (bias_rows, heads)
        )
        for grad in totals[4 * features :].reshape(2, BUCKETS, tensor_count * heads)
    ]

    def split_four(summed):
        return (
            summed[:, :width],
            summed[:, width : 2 * width],
            summed[:, 2 * width : 3 * width],
            summed[:, 3 * width :].T,
        )

    return (
        layer_output,
        grad_zero,
        gain_grads[0],
        *split_four(summed_one),
        bias_grads[0],
        gain_grads[1],
        dense_up_grad,
        dense_down_grad,
        gain_grads[2],
        *split_four(summed_two),
        bias_grads[1],
        gain_grads[3],
        expert_up_grad,
        expert_down_grad,
    )


def solution(mesh):
    attn = (P("dp", "tensor"), P("dp", "tensor"), P("dp", "tensor"), P("tensor", "dp"),
            P("dp", "tensor"))
    both = P(("dp", "tensor"))
    rows = P(("dp", "tensor"), None)
    return jax.shard_map(
        on_device,
        mesh=mesh,
        in_specs=(
            rows, P("dp", None), P("dp", None), P("dp", None),
            both, *attn,
            both, P("dp", "tensor"), P("tensor", "dp"),
            both, *attn,
            both, P("dp", None, "tensor"), P("dp", "tensor", None), rows,
        ),
        out_specs=(
            rows, rows,
            both, *attn,
            both, P("dp", "tensor"), P("tensor", "dp"),
            both, *attn,
            both, P("dp", None, "tensor"), P("dp", "tensor", None),
        ),
        check_vma=False,
    )
```

time: 992 us -> 556 us (0.56)
  waiting for transfers between devices: 472 us -> 72.2 us
  starting transfers between devices: 17.4 us -> 63.8 us
  local copies, waits for them, and re-layouts: 93.8 us -> 51 us
  matrix products: 69.8 us -> 39.5 us
  blocking collectives: 277 us -> 254 us
  Pallas kernels: 0 us -> 13 us
  other arithmetic: 33.5 us -> 44.7 us
    reduce_scatter x16 -> x0, waiting for transfers between devices: 420 us -> none  [the longest x2 77.2 us: send_block_grads(): lax.psum_scatter(query_g, 'dp', scatter_dimension=0, tiled=True)]
    unnamed x4 -> x0, blocking collectives: 55 us -> none
    psum x0 -> x1, blocking collectives: none -> 48 us  [on_device(): lax.psum(jnp.concatenate([gain_one[0], gain_dense[0], gain_two[0], expert...]
    all_to_all x4 -> x15, starting transfers between devices: 16.3 us -> 63.6 us  [the longest x11 47.8 us: swap_sum(): lax.all_to_all(blocks, axis_name, split_axis=0, concat_axis=0, tiled=True)]
    all_to_all x4 -> x15, waiting for transfers between devices: 41.7 us -> 72.2 us  [the longest x4 38.1 us: swap_blocks(): return lax.all_to_all(blocks, 'dp', split_axis=0, concat_axis=0, tiled=True)]
    all_gather x18 -> x9, blocking collectives: 222 us -> 193 us  [the longest x8 124 us: gather_rows(): return lax.all_gather(hidden.astype(BF16), 'tensor', axis=0, tiled=True)]
    dot_general x50 -> x14, matrix products: 67.4 us -> 39.5 us  [the longest x4 8.78 us: mm(): lax.dot_general(left, right, (((left_dim,), (right_dim,)), ((), ())), pre...]
    gather x6 -> x0, local copies, waits for them, and re-layouts: 16.8 us -> none  [the longest x2 4.85 us: expert_forward(): picked = returned.reshape(-1, returned.shape[3])[slot_ids]]
  transfers between devices with their start and end apart: 24 -> 18, of which waited for: 17 -> 8; matrix products, arithmetic and copies ran while one was open for 12% -> 18% of each run, Pallas kernels for 0% -> 2%
where the time goes in v1:
time: 556 us; the launch traced here: 553 us
  blocking collectives  254 us (46%)
  waiting for transfers between devices  72.2 us (13%)
  starting transfers between devices  63.8 us (11%)
  local copies, waits for them, and re-layouts  51 us (9%)
  other arithmetic  44.7 us (8%)
  matrix products  39.5 us (7%)
  between operations  14.7 us (3%)
  Pallas kernels  13 us (2%)
    all_gather x8, blocking collectives, gather_rows(): return lax.all_gather(hidden.astype(BF16), 'tensor', axis=0, tiled=True)  124 us
    all_gather x1, blocking collectives, on_device(): smalls = lax.all_gather(small[None], ('dp', 'tensor'), axis=0, tiled=True)  69.8 us
    psum x1, blocking collectives, on_device(): lax.psum(jnp.concatenate([gain_one[0], gain_dense[0], gain_two[0], expert...  48 us
    all_to_all x11, starting transfers between devices, swap_sum(): lax.all_to_all(blocks, axis_name, split_axis=0, concat_axis=0, tiled=True)  47.8 us
    all_to_all x4, waiting for transfers between devices, swap_blocks(): return lax.all_to_all(blocks, 'dp', split_axis=0, concat_axis=0, tiled=True)  38.1 us
    all_to_all x11, waiting for transfers between devices, swap_sum(): lax.all_to_all(blocks, axis_name, split_axis=0, concat_axis=0, tiled=True)  34.1 us
    unnamed x150, local copies, waits for them, and re-layouts  23.4 us
    all_to_all x4, starting transfers between devices, swap_blocks(): return lax.all_to_all(blocks, 'dp', split_axis=0, concat_axis=0, tiled=True)  15.8 us
  transfers between devices with their start and end apart: 18, of which 8 were waited for; matrix products, arithmetic and copies ran while one was open for 18% of the time, Pallas kernels for 2%

profile of v1, /device:TPU:0, one launch (start us, length us, event | category | flops | bytes accessed | tf_op | source)
XLA Modules:
  0.0 553.3 jit_solution(2328439834651777814)
XLA Ops:
  8.4 1.6 pad_maximum_fusion.1
  10.1 1.7 pad_maximum_fusion
  12.8 1.6 pad_maximum_fusion.2
  14.7 69.8 %all-gather.1 = bf16[32,1,128]{2,1,0:T(2,128)(2,1)S(1)} all-gather(bf16[1,1,128]{2,1,0:T(2,128)(2,1)S(1)} %pad_bitcast_fusion), channel_id=2, replica_groups=mesh['dp'=8,'tensor'=4] {'dp','tensor'}, dimensions={0}, use_global_device_ids=true | all-gather | bytes 8448 | tf_op jit(solution)/shard_map/all_gather | solution.py:231
  89.2 15.6 %all_gather.36.x_ref = bf16[256,768]{1,0:T(8,128)(2,1)} all-gather(bf16[64,768]{1,0:T(8,128)(2,1)} %convert_element_type.135), channel_id=1, replica_groups=mesh['dp'=8,'tensor'=4] {'tensor'}, dimensions={0}, use_global_device_ids=true | all-gather | bytes 491520 | tf_op jit(solution)/shard_map/all_gather | solution.py:183
  111.1 4.1 all-to-all-start
  115.3 9.9 %all-to-all-done = bf16[4,64,768]{2,1,0:T(8,128)(2,1)} async-done(((bf16[4,64,768]{2,1,0:T(8,128)(2,1)}), bf16[4,64,768]{2,1,0:T(8,128)(2,1)}, u32[]{:S(2)}, u32[]{:S(2)}) %all-to-all-start) | async-done | bytes 393248 | tf_op jit(solution)/shard_map/all_to_all | solution.py:188
  126.3 1.6 fusion.67
  127.9 14.9 %all_gather.39.x_ref = bf16[256,768]{1,0:T(8,128)(2,1)} all-gather(bf16[64,768]{1,0:T(8,128)(2,1)S(1)} %get-tuple-element.192), channel_id=1, replica_groups=mesh['dp'=8,'tensor'=4] {'tensor'}, dimensions={0}, use_global_device_ids=true | all-gather | bytes 491520 | tf_op jit(solution)/shard_map/all_gather | solution.py:183
  142.9 1.7 copy-done.2
  148.2 4.1 all-to-all-start.1
  154.7 2.5 fusion.72
  159.4 1.6 eq.77
  161.1 2.2 slice.109.wqkv_ref
  163.3 1.9 slice.110.wo_ref
  166.4 1.6 fusion.66
  168.1 15.6 %all_gather.41.x_ref = bf16[256,768]{1,0:T(8,128)(2,1)S(1)} all-gather(bf16[64,768]{1,0:T(8,128)(2,1)S(1)} %get-tuple-element.190), channel_id=1, replica_groups=mesh['dp'=8,'tensor'=4] {'tensor'}, dimensions={0}, use_global_device_ids=true | all-gather | bytes 491520 | tf_op jit(solution)/shard_map/all_gather | solution.py:183
  183.7 1.6 shard_map.385
  187.5 4.1 all-to-all-start.2
  192.9 1.6 eq.73
  194.5 3.1 reduce-window.6
  209.3 1.6 fusion.65
  210.9 14.8 %all_gather.43 = bf16[256,768]{1,0:T(8,128)(2,1)S(1)} all-gather(bf16[64,768]{1,0:T(8,128)(2,1)S(1)} %get-tuple-element.188), channel_id=1, replica_groups=mesh['dp'=8,'tensor'=4] {'tensor'}, dimensions={0}, use_global_device_ids=true | all-gather | bytes 491520 | tf_op jit(solution)/shard_map/all_gather | solution.py:183
  228.0 4.3 all-to-all-start.3
  233.3 14.8 %all_gather.44 = bf16[256,768]{1,0:T(8,128)(2,1)S(1)} all-gather(bf16[64,768]{1,0:T(8,128)(2,1)S(1)} %convert_element_type.154), channel_id=1, replica_groups=mesh['dp'=8,'tensor'=4] {'tensor'}, dimensions={0}, use_global_device_ids=true | all-gather | bytes 491520 | tf_op jit(solution)/shard_map/all_gather | solution.py:183
  248.3 1.8 fusion.21
  250.2 4.4 all-to-all-start.6
  254.6 4.2 fusion.15
  258.9 12.4 %all-to-all-done.6 = bf16[8,2,48,768]{3,2,1,0:T(8,128)(2,1)} async-done(((bf16[8,2,48,768]{3,2,1,0:T(8,128)(2,1)}), bf16[8,2,48,768]{3,2,1,0:T(8,128)(2,1)}, u32[]{:S(2)}, u32[]{:S(2)}) %all-to-all-start.6) | async-done | bytes 1179680 | tf_op jit(solution)/shard_map/all_to_all | solution.py:193
  271.2 4.2 fusion.5
  277.6 3.6 all-to-all-start.7
  281.2 3.1 fusion.31
  285.4 12.5 %all-to-all-done.7 = bf16[8,2,48,768]{3,2,1,0:T(8,128)(2,1)S(1)} async-done(((bf16[8,2,48,768]{3,2,1,0:T(8,128)(2,1)}), bf16[8,2,48,768]{3,2,1,0:T(8,128)(2,1)S(1)}, u32[]{:S(2)}, u32[]{:S(2)}) %all-to-all-start.7) | async-done | bytes 1179680 | tf_op jit(solution)/shard_map/all_to_all | solution.py:193
  298.9 3.6 all-to-all-start.4
  302.5 2.5 fusion.49
  306.0 13.2 %all-to-all-done.4 = bf16[8,2,48,768]{3,2,1,0:T(8,128)(2,1)S(1)} async-done(((bf16[8,2,48,768]{3,2,1,0:T(8,128)(2,1)}), bf16[8,2,48,768]{3,2,1,0:T(8,128)(2,1)S(1)}, u32[]{:S(2)}, u32[]{:S(2)}) %all-to-all-start.4) | async-done | bytes 1179680 | tf_op jit(solution)/shard_map/all_to_all | solution.py:193
  320.3 5.4 all-to-all-start.8
  325.9 2.9 multiply_reduce_fusion
  328.8 5.7 %all-to-all-done.8 = bf16[4,64,768]{2,1,0:T(8,128)(2,1)S(1)} async-done(((bf16[4,64,768]{2,1,0:T(8,128)(2,1)}), bf16[4,64,768]{2,1,0:T(8,128)(2,1)S(1)}, u32[]{:S(2)}, u32[]{:S(2)}) %all-to-all-start.8) | async-done | bytes 393248 | tf_op jit(solution)/shard_map/all_to_all | solution.py:188
  334.5 4.1 all-to-all-start.5
  338.7 1.6 fusion.64
  340.3 17.4 %all_gather.45.b_ref = bf16[256,768]{1,0:T(8,128)(2,1)S(1)} all-gather(bf16[64,768]{1,0:T(8,128)(2,1)S(1)} %get-tuple-element.186), channel_id=1, replica_groups=mesh['dp'=8,'tensor'=4] {'tensor'}, dimensions={0}, use_global_device_ids=true | all-gather | bytes 491520 | tf_op jit(solution)/shard_map/all_gather | solution.py:183
  358.7 3.0 shard_map.386
  363.5 13.1 %all_to_all.80 = bf16[4,64,768]{2,1,0:T(8,128)(2,1)} all-to-all(bf16[4,64,768]{2,1,0:T(8,128)(2,1)} %bitcast.153), channel_id=1, replica_groups=mesh['dp'=8,'tensor'=4] {'tensor'}, dimensions={0} | all-to-all | bytes 786432 | tf_op jit(solution)/shard_map/all_to_all | solution.py:188
  376.6 6.8 %all-to-all-start.15 = ((bf16[8,96,768]{2,1,0:T(8,128)(2,1)}), bf16[8,96,768]{2,1,0:T(8,128)(2,1)}, u32[]{:S(2)}, u32[]{:S(2)}) async-start(bf16[8,96,768]{2,1,0:T(8,128)(2,1)} %bitcast.148), calls=%async_computation.15 | async-start | bytes 2359296 | tf_op jit(solution)/shard_map/all_to_all | solution.py:188
  384.5 1.6 fusion.63
  386.1 15.3 %all_gather.46.b_ref = bf16[256,768]{1,0:T(8,128)(2,1)S(1)} all-gather(bf16[64,768]{1,0:T(8,128)(2,1)S(1)} %get-tuple-element.184), channel_id=1, replica_groups=mesh['dp'=8,'tensor'=4] {'tensor'}, dimensions={0}, use_global_device_ids=true | all-gather | bytes 491520 | tf_op jit(solution)/shard_map/all_gather | solution.py:183
  401.5 1.8 shard_map.387
  405.1 3.5 all-to-all-start.10
  409.1 9.2 %all-to-all-done.10 = bf16[4,64,768]{2,1,0:T(8,128)(2,1)S(1)} async-done(((bf16[4,64,768]{2,1,0:T(8,128)(2,1)}), bf16[4,64,768]{2,1,0:T(8,128)(2,1)S(1)}, u32[]{:S(2)}, u32[]{:S(2)}) %all-to-all-start.10) | async-done | bytes 393248 | tf_op jit(solution)/shard_map/all_to_all | solution.py:188
  418.3 3.8 all-to-all-start.13
  422.1 5.3 convolution_bitcast_fusion.1
  427.5 4.9 convolution_bitcast_fusion
  433.6 1.6 add.92
  435.8 1.8 fusion.74
  438.8 4.3 all-to-all-start.14
  447.9 15.1 %all_gather.47.b_ref = bf16[256,768]{1,0:T(8,128)(2,1)S(1)} all-gather(bf16[64,768]{1,0:T(8,128)(2,1)S(1)} %get-tuple-element.182), channel_id=1, replica_groups=mesh['dp'=8,'tensor'=4] {'tensor'}, dimensions={0}, use_global_device_ids=true | all-gather | bytes 491520 | tf_op jit(solution)/shard_map/all_gather | solution.py:183
  465.0 4.0 shard_map.388
  469.8 3.0 fusion.73
  472.8 3.5 all-to-all-start.11
  476.9 8.6 %all-to-all-done.11 = bf16[4,64,768]{2,1,0:T(8,128)(2,1)S(1)} async-done(((bf16[4,64,768]{2,1,0:T(8,128)(2,1)}), bf16[4,64,768]{2,1,0:T(8,128)(2,1)S(1)}, u32[]{:S(2)}, u32[]{:S(2)}) %all-to-all-start.11) | async-done | bytes 393248 | tf_op jit(solution)/shard_map/all_to_all | solution.py:188
  485.5 4.3 all-to-all-start.12
  489.8 48.0 %psum.7 = f32[3840]{0:T(1024)S(1)} all-reduce(f32[3840]{0:T(1024)S(1)} %constant_dynamic-update-slice_fusion), channel_id=1, replica_groups=mesh['dp'=8,'tensor'=4] {'dp','tensor'}, use_global_device_ids=true, to_apply=%region_16.17 | all-reduce | flops 3840 | bytes 30720 | tf_op jit(solution)/shard_map/psum | solution.py:362
  540.8 2.2 convert_reduce_fusion.1
  (246 shorter events, 73.2 us)
Async XLA Ops:
  7.2 247.4 %copy-start = (bf16[2,768,768]{2,1,0:T(8,128)(2,1)S(1)}, bf16[2,768,768]{2,1,0:T(8,128)(2,1)}, u32[]{:S(2)}) copy-start(bf16[2,768,768]{2,1,0:T(8,128)(2,1)} %param.44) | copy-start | bytes 7077892
  7.2 81.2 %copy-start.37 = (f32[2048,32]{1,0:T(8,128)S(1)}, f32[2048,32]{1,0:T(8,128)}, u32[]{:S(2)}) copy-start(f32[2048,32]{1,0:T(8,128)} %constant.70.clone) | copy-start | bytes 786436
  7.2 7.2 %copy-start.64 = (bf16[4,3]{1,0:T(4,128)(2,1)S(1)}, bf16[4,3]{1,0:T(4,128)(2,1)}, u32[]{:S(2)}) copy-start(bf16[4,3]{1,0:T(4,128)(2,1)} %param.33) | copy-start | bytes 76
  7.2 7.3 %copy-start.65 = (bf16[4,3]{1,0:T(4,128)(2,1)S(1)}, bf16[4,3]{1,0:T(4,128)(2,1)}, u32[]{:S(2)}) copy-start(bf16[4,3]{1,0:T(4,128)(2,1)} %param.42) | copy-start | bytes 76
  7.2 7.3 %copy-start.60 = (bf16[24]{0:T(256)(128)(2,1)S(1)}, bf16[24]{0:T(256)(128)(2,1)}, u32[]{:S(2)}) copy-start(bf16[24]{0:T(256)(128)(2,1)} %param.28) | copy-start | bytes 148
  7.3 7.3 %copy-start.61 = (bf16[24]{0:T(256)(128)(2,1)S(1)}, bf16[24]{0:T(256)(128)(2,1)}, u32[]{:S(2)}) copy-start(bf16[24]{0:T(256)(128)(2,1)} %param.34) | copy-start | bytes 148
  7.3 7.3 %copy-start.62 = (bf16[24]{0:T(256)(128)(2,1)S(1)}, bf16[24]{0:T(256)(128)(2,1)}, u32[]{:S(2)}) copy-start(bf16[24]{0:T(256)(128)(2,1)} %param.37) | copy-start | bytes 148
  7.3 7.3 %copy-start.63 = (bf16[24]{0:T(256)(128)(2,1)S(1)}, bf16[24]{0:T(256)(128)(2,1)}, u32[]{:S(2)}) copy-start(bf16[24]{0:T(256)(128)(2,1)} %param.43) | copy-start | bytes 148
  7.3 97.5 %all-gather.6.cloned.1.call-start = ((), (), s32[]{:S(2)}) async-start(), calls=%async_computation.16 | async-start | bytes 1327104 | tf_op jit(solution)/shard_map/all_gather | solution.py:254
  10.0 132.8 %all-gather.8.cloned.1.call-start = ((), (), s32[]{:S(2)}) async-start(), calls=%async_computation.17 | async-start | bytes 2654208 | tf_op jit(solution)/shard_map/all_gather | solution.py:254
  10.1 79.0 %copy-start.34 = (s32[1,256]{1,0:T(1,128)S(1)}, s32[1,256]{1,0:T(1,128)}, u32[]{:S(2)}) copy-start(s32[1,256]{1,0:T(1,128)} %segr_ref.7) | copy-start | bytes 3076
  11.8 149.3 %all-gather.10.cloned.1.call-start = ((), (), s32[]{:S(2)}) async-start(), calls=%async_computation.18 | async-start | bytes 1327104 | tf_op jit(solution)/shard_map/all_gather | solution.py:254
  104.8 2.5 copy-start.6
  106.2 9.0 %copy-start.51 = (f32[32,24]{1,0:T(8,128)S(1)}, f32[32,24]{1,0:T(8,128)}, u32[]{:S(2)}) copy-start(f32[32,24]{1,0:T(8,128)} %get-tuple-element.210) | copy-start | bytes 9220
  111.1 14.1 %all-to-all-start = ((bf16[4,64,768]{2,1,0:T(8,128)(2,1)}), bf16[4,64,768]{2,1,0:T(8,128)(2,1)}, u32[]{:S(2)}, u32[]{:S(2)}) async-start(bf16[4,64,768]{2,1,0:T(8,128)(2,1)} %bitcast.154), calls=%async_computation | async-start | bytes 786432 | tf_op jit(solution)/shard_map/all_to_all | solution.py:188
  142.9 1.7 copy-start.2
  145.5 7.6 %copy-start.50 = (bf16[8,1,4,3]{1,0,3,2:T(8,128)(2,1)S(1)}, bf16[8,1,4,3]{1,0,3,2:T(8,128)(2,1)}, u32[]{:S(2)}) copy-start(bf16[8,1,4,3]{1,0,3,2:T(8,128)(2,1)} %get-tuple-element.221) | copy-start | bytes 580
  148.2 17.1 %all-to-all-start.1 = ((bf16[4,64,768]{2,1,0:T(8,128)(2,1)}), bf16[4,64,768]{2,1,0:T(8,128)(2,1)}, u32[]{:S(2)}, u32[]{:S(2)}) async-start(bf16[4,64,768]{2,1,0:T(8,128)(2,1)} %bitcast.152), calls=%async_computation.1 | async-start | bytes 786432 | tf_op jit(solution)/shard_map/all_to_all | solution.py:188
  165.2 18.5 %copy-start.4 = (bf16[768,576]{1,0:T(8,128)(2,1)S(1)}, bf16[768,576]{1,0:T(8,128)(2,1)}, u32[]{:S(2)}) copy-start(bf16[768,576]{1,0:T(8,128)(2,1)} %slice.109.wqkv_ref) | copy-start | bytes 2654212
  165.2 18.5 %copy-start.10 = (bf16[768,192]{1,0:T(8,128)(2,1)S(1)}, bf16[768,192]{1,0:T(8,128)(2,1)}, u32[]{:S(2)}) copy-start(bf16[768,192]{1,0:T(8,128)(2,1)} %slice.110.wo_ref) | copy-start | bytes 884740
  183.7 1.6 copy-start.12
  187.5 20.7 %all-to-all-start.2 = ((bf16[4,64,768]{2,1,0:T(8,128)(2,1)}), bf16[4,64,768]{2,1,0:T(8,128)(2,1)}, u32[]{:S(2)}, u32[]{:S(2)}) async-start(bf16[4,64,768]{2,1,0:T(8,128)(2,1)} %bitcast.151), calls=%async_computation.2 | async-start | bytes 786432 | tf_op jit(solution)/shard_map/all_to_all | solution.py:188
  206.3 20.1 %copy-start.52 = (f32[768]{0:T(1024)S(1)}, f32[768]{0:T(1024)}, u32[]{:S(2)}) copy-start(f32[768]{0:T(1024)} %reshape.294) | copy-start | bytes 9220
  208.2 18.3 %copy-start.44 = (bf16[768,256]{1,0:T(8,128)(2,1)S(1)}, bf16[768,256]{1,0:T(8,128)(2,1)}, u32[]{:S(2)}) copy-start(bf16[768,256]{1,0:T(8,128)(2,1)} %fusion.51) | copy-start | bytes 1179652
  228.0 22.1 %all-to-all-start.3 = ((bf16[8,2,48,768]{3,2,1,0:T(8,128)(2,1)}), bf16[8,2,48,768]{3,2,1,0:T(8,128)(2,1)}, u32[]{:S(2)}, u32[]{:S(2)}) async-start(bf16[8,2,48,768]{3,2,1,0:T(8,128)(2,1)} %bitcast.156), calls=%async_computation.3 | async-start | bytes 2359296 | tf_op jit(solution)/shard_map/all_to_all | solution.py:193
  232.3 15.9 %copy-start.57 = (f32[256,2]{0,1:T(2,128)S(1)}, f32[256,2]{0,1:T(2,128)}, u32[]{:S(2)}) copy-start(f32[256,2]{0,1:T(2,128)} %param.27) | copy-start | bytes 6148
  250.2 21.1 %all-to-all-start.6 = ((bf16[8,2,48,768]{3,2,1,0:T(8,128)(2,1)}), bf16[8,2,48,768]{3,2,1,0:T(8,128)(2,1)}, u32[]{:S(2)}, u32[]{:S(2)}) async-start(bf16[8,2,48,768]{3,2,1,0:T(8,128)(2,1)} %bitcast.159), calls=%async_computation.6 | async-start | bytes 2359296 | tf_op jit(solution)/shard_map/all_to_all | solution.py:193
  277.6 20.3 %all-to-all-start.7 = ((bf16[8,2,48,768]{3,2,1,0:T(8,128)(2,1)}), bf16[8,2,48,768]{3,2,1,0:T(8,128)(2,1)S(1)}, u32[]{:S(2)}, u32[]{:S(2)}) async-start(bf16[8,2,48,768]{3,2,1,0:T(8,128)(2,1)} %copy.184), calls=%async_computation.7 | async-start | bytes 2359296 | tf_op jit(solution)/shard_map/all_to_all | solution.py:193
  285.4 17.1 %copy-start.40 = (bf16[256,768]{1,0:T(8,128)(2,1)S(1)}, bf16[256,768]{1,0:T(8,128)(2,1)}, u32[]{:S(2)}) copy-start(bf16[256,768]{1,0:T(8,128)(2,1)} %copy-done.39) | copy-start | bytes 1179652
  285.4 17.1 %copy-start.45 = (bf16[768,256]{1,0:T(8,128)(2,1)S(1)}, bf16[768,256]{1,0:T(8,128)(2,1)}, u32[]{:S(2)}) copy-start(bf16[768,256]{1,0:T(8,128)(2,1)} %fusion.51) | copy-start | bytes 1179652
  298.9 20.3 %all-to-all-start.4 = ((bf16[8,2,48,768]{3,2,1,0:T(8,128)(2,1)}), bf16[8,2,48,768]{3,2,1,0:T(8,128)(2,1)S(1)}, u32[]{:S(2)}, u32[]{:S(2)}) async-start(bf16[8,2,48,768]{3,2,1,0:T(8,128)(2,1)} %copy.182), calls=%async_computation.4 | async-start | bytes 2359296 | tf_op jit(solution)/shard_map/all_to_all | solution.py:193
  305.0 20.9 %copy-start.58 = (f32[256,2]{0,1:T(2,128)S(1)}, f32[256,2]{0,1:T(2,128)}, u32[]{:S(2)}) copy-start(f32[256,2]{0,1:T(2,128)} %param.27) | copy-start | bytes 6148
  320.3 14.3 %all-to-all-start.8 = ((bf16[4,64,768]{2,1,0:T(8,128)(2,1)}), bf16[4,64,768]{2,1,0:T(8,128)(2,1)S(1)}, u32[]{:S(2)}, u32[]{:S(2)}) async-start(bf16[4,64,768]{2,1,0:T(8,128)(2,1)} %bitcast.29), calls=%async_computation.8 | async-start | bytes 786432 | tf_op jit(solution)/shard_map/all_to_all | solution.py:188
  328.8 28.9 %copy-start.5 = (bf16[768,576]{1,0:T(8,128)(2,1)S(1)}, bf16[768,576]{1,0:T(8,128)(2,1)}, u32[]{:S(2)}) copy-start(bf16[768,576]{1,0:T(8,128)(2,1)} %slice.109.wqkv_ref) | copy-start | bytes 2654212
  328.8 28.9 %copy-start.11 = (bf16[768,192]{1,0:T(8,128)(2,1)S(1)}, bf16[768,192]{1,0:T(8,128)(2,1)}, u32[]{:S(2)}) copy-start(bf16[768,192]{1,0:T(8,128)(2,1)} %slice.110.wo_ref) | copy-start | bytes 884740
  328.8 28.9 %copy-start.13 = (bf16[256,768]{1,0:T(8,128)(2,1)S(1)}, bf16[256,768]{1,0:T(8,128)(2,1)}, u32[]{:S(2)}) copy-start(bf16[256,768]{1,0:T(8,128)(2,1)} %copy-done.12) | copy-start | bytes 1179652
  328.8 28.9 %copy-start.33 = (bf16[256,192]{1,0:T(8,128)(2,1)S(1)}, bf16[256,192]{1,0:T(8,128)(2,1)}, u32[]{:S(2)}) copy-start(bf16[256,192]{1,0:T(8,128)(2,1)} %copy-done.32) | copy-start | bytes 294916
  334.5 29.0 %all-to-all-start.5 = ((bf16[4,64,768]{2,1,0:T(8,128)(2,1)}), bf16[4,64,768]{2,1,0:T(8,128)(2,1)}, u32[]{:S(2)}, u32[]{:S(2)}) async-start(bf16[4,64,768]{2,1,0:T(8,128)(2,1)} %bitcast.162), calls=%async_computation.5 | async-start | bytes 786432 | tf_op jit(solution)/shard_map/all_to_all | solution.py:188
  363.5 13.1 %copy-start.35 = (f32[24,256]{1,0:T(8,128)}, f32[24,256]{1,0:T(8,128)S(1)}, u32[]{:S(2)}) copy-start(f32[24,256]{1,0:T(8,128)S(1)} %get-tuple-element.55) | copy-start | bytes 73732
  376.6 24.9 %copy-start.3 = (bf16[768,1536]{1,0:T(8,128)(2,1)S(1)}, bf16[768,1536]{1,0:T(8,128)(2,1)}, u32[]{:S(2)}) copy-start(bf16[768,1536]{1,0:T(8,128)(2,1)} %all-gather.8.cloned.1.call-done.w_ref) | copy-start | bytes 7077892
  376.6 28.5 %all-to-all-start.15 = ((bf16[8,96,768]{2,1,0:T(8,128)(2,1)}), bf16[8,96,768]{2,1,0:T(8,128)(2,1)}, u32[]{:S(2)}, u32[]{:S(2)}) async-start(bf16[8,96,768]{2,1,0:T(8,128)(2,1)} %bitcast.148), calls=%async_computation.15 | async-start | bytes 2359296 | tf_op jit(solution)/shard_map/all_to_all | solution.py:188
  383.3 18.1 %copy-start.15 = (bf16[256,768]{1,0:T(8,128)(2,1)S(1)}, bf16[256,768]{1,0:T(8,128)(2,1)}, u32[]{:S(2)}) copy-start(bf16[256,768]{1,0:T(8,128)(2,1)} %all_gather.39.x_ref) | copy-start | bytes 1179652
  383.3 18.1 %copy-start.19 = (f32[256,768]{1,0:T(8,128)S(1)}, f32[256,768]{1,0:T(8,128)}, u32[]{:S(2)}) copy-start(f32[256,768]{1,0:T(8,128)} %copy-done.18) | copy-start | bytes 2359300
  405.1 13.2 %all-to-all-start.10 = ((bf16[4,64,768]{2,1,0:T(8,128)(2,1)}), bf16[4,64,768]{2,1,0:T(8,128)(2,1)S(1)}, u32[]{:S(2)}, u32[]{:S(2)}) async-start(bf16[4,64,768]{2,1,0:T(8,128)(2,1)} %bitcast.149), calls=%async_computation.10 | async-start | bytes 786432 | tf_op jit(solution)/shard_map/all_to_all | solution.py:188
  418.3 9.2 %copy-start.43 = (bf16[4,64,768]{2,1,0:T(8,128)(2,1)}, bf16[4,64,768]{2,1,0:T(8,128)(2,1)S(1)}, u32[]{:S(2)}) copy-start(bf16[4,64,768]{2,1,0:T(8,128)(2,1)S(1)} %all-to-all-done.10) | copy-start | bytes 1179652
  418.3 20.5 %all-to-all-start.13 = ((bf16[8,96,768]{2,1,0:T(8,128)(2,1)}), bf16[8,96,768]{2,1,0:T(8,128)(2,1)S(1)}, u32[]{:S(2)}, u32[]{:S(2)}) async-start(bf16[8,96,768]{2,1,0:T(8,128)(2,1)} %bitcast.147), calls=%async_computation.13 | async-start | bytes 2359296 | tf_op jit(solution)/shard_map/all_to_all | solution.py:188
  422.1 5.4 copy-start.66
  427.5 4.9 copy-start.36
  432.4 3.4 copy-start.38
  438.8 5.8 %copy-start.41 = (bf16[8,96,768]{2,1,0:T(8,128)(2,1)}, bf16[8,96,768]{2,1,0:T(8,128)(2,1)S(1)}, u32[]{:S(2)}) copy-start(bf16[8,96,768]{2,1,0:T(8,128)(2,1)S(1)} %all-to-all-done.13) | copy-start | bytes 3538948
  438.8 33.9 %all-to-all-start.14 = ((bf16[8,96,768]{2,1,0:T(8,128)(2,1)}), bf16[8,96,768]{2,1,0:T(8,128)(2,1)}, u32[]{:S(2)}, u32[]{:S(2)}) async-start(bf16[8,96,768]{2,1,0:T(8,128)(2,1)} %bitcast.36), calls=%async_computation.14 | async-start | bytes 2359296 | tf_op jit(solution)/shard_map/all_to_all | solution.py:188
  443.1 4.1 copy-start.48
  444.6 18.5 %copy-start.7 = (bf16[256,768]{1,0:T(8,128)(2,1)S(1)}, bf16[256,768]{1,0:T(8,128)(2,1)}, u32[]{:S(2)}) copy-start(bf16[256,768]{1,0:T(8,128)(2,1)} %all_gather.36.x_ref) | copy-start | bytes 1179652
  444.6 18.5 %copy-start.9 = (bf16[768,192]{1,0:T(8,128)(2,1)S(1)}, bf16[768,192]{1,0:T(8,128)(2,1)}, u32[]{:S(2)}) copy-start(bf16[768,192]{1,0:T(8,128)(2,1)} %copy-done.8) | copy-start | bytes 884740
  469.7 6.6 %copy-start.59 = (f32[4]{0:T(128)S(1)}, f32[4]{0:T(128)}, u32[]{:S(2)}) copy-start(f32[4]{0:T(128)} %compare_convert_fusion) | copy-start | bytes 52
  469.7 7.1 %copy-start.53 = (f32[3840]{0:T(1024)S(1)}, f32[3840]{0:T(1024)}, u32[]{:S(2)}) copy-start(f32[3840]{0:T(1024)} %custom-call) | copy-start | bytes 46084
  469.7 7.1 %copy-start.55 = (f32[768]{0:T(1024)S(1)}, f32[768]{0:T(1024)}, u32[]{:S(2)}) copy-start(f32[768]{0:T(1024)} %reduce.3) | copy-start | bytes 9220
  469.7 7.1 %copy-start.54 = (f32[768]{0:T(1024)S(1)}, f32[768]{0:T(1024)}, u32[]{:S(2)}) copy-start(f32[768]{0:T(1024)} %reduce.4) | copy-start | bytes 9220
  469.7 7.2 %copy-start.56 = (f32[768]{0:T(1024)S(1)}, f32[768]{0:T(1024)}, u32[]{:S(2)}) copy-start(f32[768]{0:T(1024)} %get-tuple-element.180) | copy-start | bytes 9220
  472.8 12.8 %all-to-all-start.11 = ((bf16[4,64,768]{2,1,0:T(8,128)(2,1)}), bf16[4,64,768]{2,1,0:T(8,128)(2,1)S(1)}, u32[]{:S(2)}, u32[]{:S(2)}) async-start(bf16[4,64,768]{2,1,0:T(8,128)(2,1)} %bitcast.150), calls=%async_computation.11 | async-start | bytes 786432 | tf_op jit(solution)/shard_map/all_to_all | solution.py:188
  476.3 63.7 %copy-start.42 = (bf16[8,96,768]{2,1,0:T(8,128)(2,1)S(1)}, bf16[8,96,768]{2,1,0:T(8,128)(2,1)}, u32[]{:S(2)}) copy-start(bf16[8,96,768]{2,1,0:T(8,128)(2,1)} %copy-done.41) | copy-start | bytes 3538948
  485.5 58.2 %all-to-all-start.12 = ((bf16[8,96,768]{2,1,0:T(8,128)(2,1)}), bf16[8,96,768]{2,1,0:T(8,128)(2,1)}, u32[]{:S(2)}, u32[]{:S(2)}) async-start(bf16[8,96,768]{2,1,0:T(8,128)(2,1)} %bitcast.33), calls=%async_computation.12 | async-start | bytes 2359296 | tf_op jit(solution)/shard_map/all_to_all | solution.py:188
  540.0 3.1 copy-start.49
  543.0 3.8 copy-start.1
  (22 other events, 19.6 us)
Sparse Core Ops, SparseCore 0:
  10.5 26.6 all-gather.5
  39.7 28.8 all-gather.7
  71.1 23.9 all-gather.9

commit v2 on v1

--- a/solution.py
+++ b/solution.py
@@ -1,3 +1,4 @@
+import functools
 import math
 
 import jax
@@ -81,12 +82,13 @@
     return exp_scores / jnp.sum(exp_scores, axis=-1, keepdims=True)
 
 
-def attn_forward_kernel(x_ref, g_ref, wqkv_ref, wo_ref, band_ref, segr_ref, segc_ref,
+def attn_forward_kernel(x_ref, g_ref, w_ref, band_ref, segr_ref, segc_ref,
                         qkv_ref, o_ref, part_ref):
     normed, _, _ = norm_rows(x_ref[...], g_ref[...])
-    qkv = mm(normed, wqkv_ref[...]).astype(BF16)
+    width = o_ref.shape[1]
+    weights = w_ref[...]
+    qkv = mm(normed, weights[:, : 3 * width]).astype(BF16)
     qkv_ref[...] = qkv
-    width = o_ref.shape[1]
     allowed = allowed_pairs(segr_ref[...], segc_ref[...])
     mixed = []
     for head in range(width // DH):
@@ -100,17 +102,18 @@
         mixed.append(mm(shares, qkv[:, 2 * width + lo : 2 * width + lo + DH]).astype(BF16))
     mixed = jnp.concatenate(mixed, axis=1)
     o_ref[...] = mixed
-    part_ref[...] = mm(mixed, wo_ref[...], 1, 1).astype(BF16)
-
-
-def attn_backward_kernel(b_ref, x_ref, g_ref, wqkv_ref, wo_ref, band_ref, segr_ref, segc_ref,
+    part_ref[...] = mm(mixed, weights[:, 3 * width :], 1, 1).astype(BF16)
+
+
+def attn_backward_kernel(b_ref, x_ref, g_ref, w_ref, band_ref, segr_ref, segc_ref,
                          qkv_ref, o_ref, wg_ref, part_ref, gain_ref, bandg_ref):
     width = o_ref.shape[1]
     normed, normal, inv_rms = norm_rows(x_ref[...], g_ref[...])
     grad_rows = b_ref[...]
     mixed = o_ref[...]
     qkv = qkv_ref[...]
-    grad_mixed = mm(grad_rows, wo_ref[...]).astype(BF16)
+    weights = w_ref[...]
+    grad_mixed = mm(grad_rows, weights[:, 3 * width :]).astype(BF16)
     allowed = allowed_pairs(segr_ref[...], segc_ref[...])
     length = qkv.shape[0]
     inv_root = 1.0 / math.sqrt(DH)
@@ -141,10 +144,10 @@
     wg_ref[...] = jnp.concatenate(
         [mm(normed, grad_qkv, 0, 0).astype(BF16), mm(grad_rows, mixed, 0, 0).astype(BF16)], axis=1
     )
-    grad_normed = mm(grad_qkv, wqkv_ref[...], 1, 1)
+    grad_normed = mm(grad_qkv, weights[:, : 3 * width], 1, 1)
     grad_part, gain_grad = norm_back(grad_normed, normal, inv_rms, g_ref[...])
     part_ref[...] = grad_part.astype(BF16)
-    gain_ref[...] = gain_grad
+    gain_ref[...] = jnp.broadcast_to(gain_grad, gain_ref.shape)
 
 
 def dense_forward_kernel(x_ref, g_ref, w_ref, pre_ref, part_ref):
@@ -168,7 +171,7 @@
     grad_normed = mm(grad_pre, w_ref[:, :hidden], 1, 1)
     grad_part, gain_grad = norm_back(grad_normed, normal, inv_rms, g_ref[...])
     part_ref[...] = grad_part.astype(BF16)
-    gain_ref[...] = gain_grad
+    gain_ref[...] = jnp.broadcast_to(gain_grad, gain_ref.shape)
 
 
 def call(kernel, outs, *args):
@@ -179,8 +182,129 @@
     )(*args)
 
 
-def gather_rows(hidden):
-    return lax.all_gather(hidden.astype(BF16), "tensor", axis=0, tiled=True)
+def greet_peers(count):
+    me = lax.axis_index("tensor")
+    barrier = pltpu.get_barrier_semaphore()
+    for offset in range(1, count):
+        pl.semaphore_signal(
+            barrier, inc=1, device_id={"tensor": lax.rem(me + offset, count)},
+            device_id_type=pl.DeviceIdType.MESH,
+        )
+    pl.semaphore_wait(barrier, count - 1)
+    return me
+
+
+def remote(source, target, send_sem, recv_sem, peer):
+    return pltpu.make_async_remote_copy(
+        src_ref=source, dst_ref=target, send_sem=send_sem, recv_sem=recv_sem,
+        device_id={"tensor": peer}, device_id_type=pl.DeviceIdType.MESH,
+    )
+
+
+def gather_kernel(count, x_ref, g_ref, s_ref, xo_ref, go_ref, so_ref, send_sem, recv_sem):
+    me = greet_peers(count)
+    block = x_ref.shape[0]
+    own = pl.ds(pl.multiple_of(me * block, block), block)
+    xo_ref[own, :] = x_ref[...].astype(BF16)
+    go_ref[own, :] = g_ref[...].astype(BF16)
+    so_ref[pl.ds(me, 1)] = s_ref[...][None]
+    copies = []
+    for kind, (source, target) in enumerate([
+        (s_ref, so_ref.at[me]),
+        (xo_ref.at[own, :], xo_ref.at[own, :]),
+        (go_ref.at[own, :], go_ref.at[own, :]),
+    ]):
+        for offset in range(1, count):
+            copy = remote(source, target, send_sem.at[kind, offset], recv_sem.at[kind, offset],
+                          lax.rem(me + offset, count))
+            copy.start()
+            copies.append(copy)
+    for copy in copies:
+        copy.wait()
+
+
+def boundary_kernel(count, with_gain, spread, *refs):
+    refs = list(refs)
+    part_ref, resid_ref = refs[:2]
+    refs = refs[2:]
+    gain_ref = refs.pop(0) if with_gain else None
+    out_ref = refs.pop(0)
+    rows_ref = refs.pop(0) if spread else None
+    gain_out = refs.pop(0) if with_gain else None
+    land = refs.pop(0)
+    gain_land = refs.pop(0) if with_gain else None
+    send_sem, recv_sem = refs
+    me = greet_peers(count)
+    block = out_ref.shape[0]
+    own = pl.ds(pl.multiple_of(me * block, block), block)
+    copies, gain_copies = [], []
+    for offset in range(1, count):
+        peer = lax.rem(me + offset, count)
+        copy = remote(
+            part_ref.at[pl.ds(pl.multiple_of(peer * block, block), block), :],
+            land.at[offset - 1], send_sem.at[0, offset], recv_sem.at[0, offset], peer,
+        )
+        copy.start()
+        copies.append(copy)
+    if with_gain:
+        for offset in range(1, count):
+            copy = remote(gain_ref, gain_land.at[offset - 1], send_sem.at[1, offset],
+                          recv_sem.at[1, offset], lax.rem(me + offset, count))
+            copy.start()
+            gain_copies.append(copy)
+    total = part_ref[own, :].astype(F32)
+    for offset, copy in enumerate(copies):
+        copy.wait_recv()
+        total = total + land[offset].astype(F32)
+    total = resid_ref[...] + total
+    out_ref[...] = total
+    if spread:
+        rows_ref[own, :] = total.astype(BF16)
+        for offset in range(1, count):
+            copy = remote(rows_ref.at[own, :], rows_ref.at[own, :], send_sem.at[2, offset],
+                          recv_sem.at[2, offset], lax.rem(me + offset, count))
+            copy.start()
+            gain_copies.append(copy)
+    for copy in copies:
+        copy.wait_send()
+    for copy in gain_copies:
+        copy.wait()
+    if with_gain:
+        gain_total = gain_ref[...]
+        for offset in range(count - 1):
+            gain_total = gain_total + gain_land[offset]
+        gain_out[...] = gain_total
+
+
+def comm_call(kernel, number, outs, scratch, *args):
+    vmem = pl.BlockSpec(memory_space=pltpu.VMEM)
+    return pl.pallas_call(
+        kernel,
+        out_shape=[jax.ShapeDtypeStruct(shape, dtype) for shape, dtype in outs],
+        in_specs=[vmem] * len(args),
+        out_specs=[vmem] * len(outs),
+        scratch_shapes=scratch,
+        compiler_params=pltpu.CompilerParams(collective_id=number, has_side_effects=True),
+    )(*args)
+
+
+def boundary(number, part, resid, gain=None, spread=True):
+    count = lax.axis_size("tensor")
+    block, features = resid.shape
+    outs = [((block, features), F32)]
+    if spread:
+        outs.append((part.shape, BF16))
+    scratch = [pltpu.VMEM((count - 1, block, features), BF16)]
+    args = [part, resid]
+    if gain is not None:
+        outs.append((gain.shape, F32))
+        scratch.append(pltpu.VMEM((count - 1, *gain.shape), F32))
+        args.append(gain)
+    scratch += [pltpu.SemaphoreType.DMA((3, count)), pltpu.SemaphoreType.DMA((3, count))]
+    return comm_call(
+        functools.partial(boundary_kernel, count, gain is not None, spread),
+        number, outs, scratch, *args,
+    )
 
 
 def swap_sum(parts, axis_name, count):
@@ -197,10 +321,12 @@
     length, top_count = routes.shape
     flat_routes = routes.reshape(-1)
     onehot = (flat_routes[:, None] == jnp.arange(expert_count, dtype=jnp.int32)[None, :]).astype(
-        jnp.int32
-    )
-    before = jnp.cumsum(onehot, axis=0) - onehot
-    slot_ids = flat_routes * capacity + jnp.sum(onehot * before, axis=1)
+        BF16
+    )
+    pairs = jnp.arange(length * top_count, dtype=jnp.int32)
+    before = mm((pairs[:, None] > pairs[None, :]).astype(BF16), onehot)
+    earlier = jnp.sum(onehot.astype(F32) * before, axis=1).astype(jnp.int32)
+    slot_ids = flat_routes * capacity + earlier
     return slot_ids.reshape(length, top_count)
 
 
@@ -212,7 +338,7 @@
     second_expert_gain, expert_up, expert_down, output_grad,
 ):
     dp_count, tensor_count = lax.axis_size("dp"), lax.axis_size("tensor")
-    dp_index, tensor_index = lax.axis_index("dp"), lax.axis_index("tensor")
+    tensor_index = lax.axis_index("tensor")
     length = segments.shape[1]
     features = layer_input.shape[1]
     width = first_query.shape[1]
@@ -228,7 +354,15 @@
     )
     pad = (-small.shape[0]) % 128
     small = jnp.pad(small, (0, pad))
-    smalls = lax.all_gather(small[None], ("dp", "tensor"), axis=0, tiled=True)
+    rows_zero, out_grad_rows, smalls = comm_call(
+        functools.partial(gather_kernel, tensor_count), 1,
+        [((length, features), BF16), ((length, features), BF16),
+         ((tensor_count, 8, small.shape[0]), F32)],
+        [pltpu.SemaphoreType.DMA((3, tensor_count)), pltpu.SemaphoreType.DMA((3, tensor_count))],
+        layer_input, output_grad,
+        jnp.broadcast_to(small.astype(F32)[None], (8, small.shape[0])),
+    )
+    smalls = lax.all_gather(smalls[:, 0, :].astype(BF16), "dp", axis=0, tiled=True)
     gains = [
         smalls[:, k * piece : (k + 1) * piece].astype(F32).reshape(1, features) for k in range(4)
     ]
@@ -260,25 +394,21 @@
     seg_col = segments.reshape(length, 1)
 
     def attn_forward(x_rows, gain, weights, band):
-        wqkv, wo = weights[:, : 3 * width], weights[:, 3 * width :]
         qkv, mixed, part = call(
             attn_forward_kernel,
             [((length, 3 * width), BF16), ((length, width), BF16), ((length, features), BF16)],
-            x_rows, gain, wqkv, wo, band, seg_row, seg_col,
-        )
-        return part, (x_rows, gain, wqkv, wo, band, qkv, mixed)
+            x_rows, gain, weights, band, seg_row, seg_col,
+        )
+        return part, (x_rows, gain, weights, band, qkv, mixed)
 
     def attn_backward(grad_rows, saved):
-        x_rows, gain, wqkv, wo, band, qkv, mixed = saved
+        x_rows, gain, weights, band, qkv, mixed = saved
         return call(
             attn_backward_kernel,
-            [((features, 4 * width), BF16), ((length, features), BF16), ((1, features), F32),
+            [((features, 4 * width), BF16), ((length, features), BF16), ((8, features), F32),
              ((heads * 8, length), F32)],
-            grad_rows, x_rows, gain, wqkv, wo, band, seg_row, seg_col, qkv, mixed,
-        )
-
-    def collect(part):
-        return swap_sum(part, "tensor", tensor_count)
+            grad_rows, x_rows, gain, weights, band, seg_row, seg_col, qkv, mixed,
+        )
 
     top_count = routes.shape[1]
     local_experts = expert_up.shape[0]
@@ -291,23 +421,21 @@
     place_rows = place.reshape(slots, top_count, length).sum(axis=1)
     sent_shape = (dp_count, local_experts, capacity, features)
 
-    out_grad_rows = gather_rows(output_grad)
     scaled = (gate_weights.T[:, :, None] * out_grad_rows.astype(F32)[None]).astype(BF16)
     sent_grad = mm(place, scaled.reshape(top_count * length, features)).astype(BF16)
     arrived_grad = swap_blocks(sent_grad.reshape(sent_shape))
 
-    part, saved_one = attn_forward(gather_rows(layer_input), gains[0], weights_one, bands[0])
-    hidden_one = layer_input + collect(part)
-    rows_one = gather_rows(hidden_one)
+    part, saved_one = attn_forward(rows_zero, gains[0], weights_one, bands[0])
+    hidden_one, rows_one = boundary(2, part, layer_input)
     pre_act, part = call(
         dense_forward_kernel,
         [((length, hidden), F32), ((length, features), BF16)],
         rows_one, gains[1], weights_dense,
     )
-    hidden_two = hidden_one + collect(part)
-    part, saved_three = attn_forward(gather_rows(hidden_two), gains[2], weights_two, bands[1])
-    hidden_three = hidden_two + collect(part)
-    rows_three = gather_rows(hidden_three)
+    part, arrived_grad = lax.optimization_barrier((part, arrived_grad))
+    hidden_two, rows_two = boundary(2, part, hidden_one)
+    part, saved_three = attn_forward(rows_two, gains[2], weights_two, bands[1])
+    hidden_three, rows_three = boundary(2, part, hidden_two)
     normed, normal, inv_rms = norm_rows(rows_three, gains[3])
     arrived = swap_blocks(mm(place_rows, normed).astype(BF16).reshape(sent_shape))
     pre_expert = jnp.einsum("secd,edf->secf", arrived, expert_up, preferred_element_type=F32)
@@ -322,7 +450,10 @@
     grad_back = swap_blocks(grad_sent).reshape(slots, features)
     grad_normed = mm(place_rows, grad_back, 0, 0)
     grad_part, expert_gain_grad = norm_back(grad_normed, normal, inv_rms, gains[3])
-    grad_three = output_grad + collect(grad_part)
+    grad_three, grad_rows_three, gain_expert = boundary(
+        3, grad_part.astype(BF16), output_grad,
+        jnp.broadcast_to(expert_gain_grad, (8, features)),
+    )
 
     active = gelu_value(pre_expert).astype(BF16)
     expert_rows = jnp.einsum(
@@ -331,50 +462,49 @@
     returned = swap_blocks(expert_rows).reshape(slots, features)
     picked = mm(place, returned, 0, 0).reshape(top_count, length, features)
     combined = jnp.sum(picked * gate_weights.T[:, :, None], axis=0)
-    layer_output = hidden_three + collect(combined)
+    (layer_output,) = boundary(4, combined.astype(BF16), hidden_three, spread=False)
     expert_down_grad = jnp.einsum("secf,secd->efd", active, arrived_grad, preferred_element_type=F32)
     expert_up_grad = jnp.einsum("secd,secf->edf", arrived, grad_pre, preferred_element_type=F32)
 
-    wg_two, part, gain_two, band_grad_two = attn_backward(gather_rows(grad_three), saved_three)
+    wg_two, part, gain_two, band_grad_two = attn_backward(grad_rows_three, saved_three)
     summed_two = swap_sum(wg_two, "dp", dp_count)
-    grad_two = grad_three + collect(part)
+    grad_two, grad_rows_two, gain_two = boundary(3, part, grad_three, gain_two)
     up_wg, down_wg, part, gain_dense = call(
         dense_backward_kernel,
         [((features, hidden), BF16), ((features, hidden), BF16), ((length, features), BF16),
-         ((1, features), F32)],
-        gather_rows(grad_two), rows_one, gains[1], weights_dense, pre_act,
+         ((8, features), F32)],
+        grad_rows_two, rows_one, gains[1], weights_dense, pre_act,
     )
     dense_up_grad = swap_sum(up_wg, "dp", dp_count)
     dense_down_grad = swap_sum(down_wg, "dp", dp_count).T
-    grad_one = grad_two + collect(part)
-    wg_one, part, gain_one, band_grad_one = attn_backward(gather_rows(grad_one), saved_one)
+    grad_one, grad_rows_one, gain_dense = boundary(3, part, grad_two, gain_dense)
+    wg_one, part, gain_one, band_grad_one = attn_backward(grad_rows_one, saved_one)
     summed_one = swap_sum(wg_one, "dp", dp_count)
-    grad_zero = grad_one + collect(part)
-
-    mine = (jnp.arange(tensor_count) == tensor_index).astype(F32)
-
-    def spread_bias(band_grad):
+    grad_zero, gain_one = boundary(5, part, grad_one, gain_one, spread=False)
+
+    def bias_block(band_grad):
         grad = jnp.dot(
             table.T, band_grad.reshape(heads, 8 * length).T, precision=lax.Precision.HIGHEST
         )
-        return (grad[:, None, :] * mine[None, :, None]).reshape(-1)
-
-    totals = lax.psum(
-        jnp.concatenate(
-            [gain_one[0], gain_dense[0], gain_two[0], expert_gain_grad[0],
-             spread_bias(band_grad_one), spread_bias(band_grad_two)]
-        ),
-        ("dp", "tensor"),
-    )
-    own = (dp_index * tensor_count + tensor_index) * piece
-    gain_grads = [
-        lax.dynamic_slice_in_dim(totals, k * features + own, piece) for k in range(4)
-    ]
+        return grad.reshape(dp_count, bias_rows * heads)
+
+    def gain_block(gain_sum):
+        block = gain_sum[0].reshape(dp_count, tensor_count, piece)
+        return lax.dynamic_index_in_dim(block, tensor_index, 1, keepdims=False)
+
+    sent_small = jnp.concatenate(
+        [gain_block(gain) for gain in (gain_one, gain_dense, gain_two, gain_expert)]
+        + [bias_block(band_grad_one), bias_block(band_grad_two)],
+        axis=1,
+    )
+    sent_small = jnp.pad(sent_small, ((0, 0), (0, pad)))
+    totals = jnp.sum(
+        lax.all_to_all(sent_small, "dp", split_axis=0, concat_axis=0, tiled=True), axis=0
+    )
+    gain_grads = [totals[k * piece : (k + 1) * piece] for k in range(4)]
     bias_grads = [
-        lax.dynamic_slice(
-            grad, (dp_index * bias_rows, tensor_index * heads), (bias_rows, heads)
-        )
-        for grad in totals[4 * features :].reshape(2, BUCKETS, tensor_count * heads)
+        totals[4 * piece + k * bias_rows * heads :][: bias_rows * heads].reshape(bias_rows, heads)
+        for k in range(2)
     ]
 
     def split_four(summed):

time: 556 us -> 479 us (0.86)
  Pallas kernels: 13 us -> 214 us
  blocking collectives: 254 us -> 69.4 us
  starting transfers between devices: 63.8 us -> 25.3 us
  waiting for transfers between devices: 72.2 us -> 35.1 us
  other arithmetic: 44.7 us -> 15.7 us
  local copies, waits for them, and re-layouts: 51 us -> 65.5 us
    pallas_call x0 -> x9, Pallas kernels: none -> 199 us  [comm_call(): pl.pallas_call(kernel, out_shape=[jax.ShapeDtypeStruct(shape, dtype) for...]
    all_gather x9 -> x1, blocking collectives: 193 us -> 22 us  [on_device(): lax.all_gather(smalls[:, 0, :].astype(BF16), 'dp', axis=0, tiled=True)]
    psum x1 -> x0, blocking collectives: 48 us -> none  [on_device(): lax.psum(jnp.concatenate([gain_one[0], gain_dense[0], gain_two[0], expert...]
    all_to_all x11 -> x3, starting transfers between devices: 47.8 us -> 12.2 us  [swap_sum(): lax.all_to_all(blocks, axis_name, split_axis=0, concat_axis=0, tiled=True)]
    all_to_all x0 -> x2, blocking collectives: none -> 27.6 us  [the longest x1 19.3 us: swap_blocks(): return lax.all_to_all(blocks, 'dp', split_axis=0, concat_axis=0, tiled=True)]
    all_to_all x4 -> x3, waiting for transfers between devices: 38.1 us -> 12.6 us  [swap_blocks(): return lax.all_to_all(blocks, 'dp', split_axis=0, concat_axis=0, tiled=True)]
    unnamed x150 -> x156, local copies, waits for them, and re-layouts: 23.4 us -> 41.1 us
    convert_element_type x11 -> x3, other arithmetic: 14.2 us -> 1.79 us  [the longest x1 1.78 us: on_device(): grad_part.astype(BF16)]
  transfers between devices with their start and end apart: 18 -> 9, of which waited for: 8 -> 3; matrix products, arithmetic and copies ran while one was open for 18% -> 14% of each run, Pallas kernels for 2% -> 40%
where the time goes in v2:
time: 479 us; the launch traced here: 476 us
  Pallas kernels  214 us (45%)
  blocking collectives  69.4 us (14%)
  local copies, waits for them, and re-layouts  65.5 us (14%)
  matrix products  36.9 us (8%)
  waiting for transfers between devices  35.1 us (7%)
  starting transfers between devices  25.3 us (5%)
  other arithmetic  15.7 us (3%)
  between operations  14.6 us (3%)
    pallas_call x9, Pallas kernels, comm_call(): pl.pallas_call(kernel, out_shape=[jax.ShapeDtypeStruct(shape, dtype) for...  199 us
    unnamed x156, local copies, waits for them, and re-layouts  41.1 us
    all_to_all x3, waiting for transfers between devices, swap_sum(): lax.all_to_all(blocks, axis_name, split_axis=0, concat_axis=0, tiled=True)  22.4 us
    all_gather x1, blocking collectives, on_device(): lax.all_gather(smalls[:, 0, :].astype(BF16), 'dp', axis=0, tiled=True)  22 us
    all_to_all x1, blocking collectives, swap_sum(): lax.all_to_all(blocks, axis_name, split_axis=0, concat_axis=0, tiled=True)  19.8 us
    all_to_all x1, blocking collectives, swap_blocks(): return lax.all_to_all(blocks, 'dp', split_axis=0, concat_axis=0, tiled=True)  19.3 us
    pallas_call x6, Pallas kernels, call(): pl.pallas_call(kernel, out_shape=[jax.ShapeDtypeStruct(shape, dtype) for...  14.6 us
    all_to_all x3, starting transfers between devices, swap_blocks(): return lax.all_to_all(blocks, 'dp', split_axis=0, concat_axis=0, tiled=True)  12.9 us
  transfers between devices with their start and end apart: 9, of which 3 were waited for; matrix products, arithmetic and copies ran while one was open for 14% of the time, Pallas kernels for 40%

profile of v2, /device:TPU:0, one launch (start us, length us, event | category | flops | bytes accessed | tf_op | source)
XLA Modules:
  0.0 476.4 jit_solution(5827915028558301970)
XLA Ops:
  8.4 1.6 pad_maximum_fusion.1
  10.1 1.7 pad_maximum_fusion
  15.4 23.4 %shard_map.383 = (bf16[256,768]{1,0:T(8,128)(2,1)}, bf16[256,768]{1,0:T(8,128)(2,1)}, f32[4,8,128]{2,1,0:T(8,128)}) custom-call(f32[64,768]{1,0:T(8,128)} %refs_1_.2, f32[64,768]{1,0:T(8,128)} %refs_1_.3, f32[8,128]{1,0:T(8,128)} %broadcast_in_dim.4.s_ref), custom_call_target="tpu_custom_call" | custom-call | tf_op jit(solution)/shard_map/pallas_call | solution.py:281
  38.7 1.0 convert_element_type.99
  40.0 1.8 fusion.21
  41.8 4.4 all-to-all-start
  47.1 22.0 %all-gather = bf16[32,1,128]{2,1,0:T(2,128)(2,1)S(1)} all-gather(bf16[4,1,128]{2,1,0:T(2,128)(2,1)S(1)} %slice.131), channel_id=2, replica_groups=mesh['dp'=8,'tensor'=4] {'dp'}, dimensions={0}, use_global_device_ids=true | all-gather | bytes 9216 | tf_op jit(solution)/shard_map/all_gather | solution.py:365
  70.4 1.8 fusion.65
  72.3 1.9 fusion.64
  75.1 1.3 copy-done.3
  76.3 1.6 shard_map.384
  80.0 22.4 %shard_map.385 = (f32[64,768]{1,0:T(8,128)}, bf16[256,768]{1,0:T(8,128)(2,1)}) custom-call(bf16[256,768]{1,0:T(8,128)(2,1)} %copy-done.27, f32[64,768]{1,0:T(8,128)} %refs_1_.2), custom_call_target="tpu_custom_call" | custom-call | tf_op jit(solution)/shard_map/pallas_call | solution.py:281
  102.5 1.7 copy-done.1
  107.8 24.2 %shard_map.387 = (f32[64,768]{1,0:T(8,128)}, bf16[256,768]{1,0:T(8,128)(2,1)}) custom-call(bf16[256,768]{1,0:T(8,128)(2,1)} %copy-done.25, f32[64,768]{1,0:T(8,128)} %get-tuple-element.69.refs_1_), custom_call_target="tpu_custom_call" | custom-call | tf_op jit(solution)/shard_map/pallas_call | solution.py:281
  132.1 1.3 copy-done.5
  134.3 1.6 shard_map.388
  138.1 23.3 %shard_map.389 = (f32[64,768]{1,0:T(8,128)}, bf16[256,768]{1,0:T(8,128)(2,1)}) custom-call(bf16[256,768]{1,0:T(8,128)(2,1)} %copy-done.26, f32[64,768]{1,0:T(8,128)} %get-tuple-element.72.refs_1_), custom_call_target="tpu_custom_call" | custom-call | tf_op jit(solution)/shard_map/pallas_call | solution.py:281
  161.3 1.2 fusion.51
  162.5 1.6 convolution_convert_fusion
  164.1 19.3 %all_to_all.49 = bf16[8,2,48,768]{3,2,1,0:T(8,128)(2,1)S(1)} all-to-all(bf16[8,2,48,768]{3,2,1,0:T(8,128)(2,1)S(1)} %bitcast.125), channel_id=1, replica_groups=mesh['dp'=8,'tensor'=4] {'dp'}, dimensions={0} | all-to-all | bytes 2359296 | tf_op jit(solution)/shard_map/all_to_all | solution.py:317
  183.4 2.2 fusion.15
  185.6 3.0 fusion.5
  188.6 1.1 fusion.28
  189.7 1.2 copy.174
  190.9 4.3 all-to-all-start.3
  195.2 3.1 fusion.31
  198.3 1.1 copy.172
  199.4 12.6 %all-to-all-done.3 = bf16[8,2,48,768]{3,2,1,0:T(8,128)(2,1)} async-done(((bf16[8,2,48,768]{3,2,1,0:T(8,128)(2,1)}), bf16[8,2,48,768]{3,2,1,0:T(8,128)(2,1)}, u32[]{:S(2)}, u32[]{:S(2)}) %all-to-all-start.3) | async-done | bytes 1179680 | tf_op jit(solution)/shard_map/all_to_all | solution.py:317
  212.0 4.3 all-to-all-start.2
  216.3 1.9 fusion.50
  218.3 1.8 fusion.49.refs_0_
  220.7 25.3 %shard_map.391 = (f32[64,768]{1,0:T(8,128)}, bf16[256,768]{1,0:T(8,128)(2,1)}, f32[8,768]{1,0:T(8,128)}) custom-call(bf16[256,768]{1,0:T(8,128)(2,1)} %fusion.49.refs_0_, f32[64,768]{1,0:T(8,128)} %refs_1_.3, f32[8,768]{1,0:T(8,128)} %broadcast_in_dim.5.refs_2_), custom_call_target="tpu_custom_call" | custom-call | tf_op jit(solution)/shard_map/pallas_call | solution.py:281
  246.0 1.3 slice_reduce_fusion
  247.3 1.4 reshape_squeeze.15
  254.2 4.0 shard_map.392
  260.2 25.7 %shard_map.393 = (f32[64,768]{1,0:T(8,128)}, bf16[256,768]{1,0:T(8,128)(2,1)}, f32[8,768]{1,0:T(8,128)}) custom-call(bf16[256,768]{1,0:T(8,128)(2,1)} %copy-done.22, f32[64,768]{1,0:T(8,128)} %get-tuple-element.80.refs_1_, f32[8,768]{1,0:T(8,128)} %copy-done.42), custom_call_target="tpu_custom_call" | custom-call | tf_op jit(solution)/shard_map/pallas_call | solution.py:281
  287.4 1.7 copy-done.2
  290.0 1.1 copy-done.19
  292.2 3.2 shard_map.394
  296.7 24.2 %shard_map.395 = (f32[64,768]{1,0:T(8,128)}, bf16[256,768]{1,0:T(8,128)(2,1)}, f32[8,768]{1,0:T(8,128)}) custom-call(bf16[256,768]{1,0:T(8,128)(2,1)} %copy-done.24, f32[64,768]{1,0:T(8,128)} %get-tuple-element.85.refs_1_, f32[8,768]{1,0:T(8,128)} %copy-done.44), custom_call_target="tpu_custom_call" | custom-call | tf_op jit(solution)/shard_map/pallas_call | solution.py:281
  327.9 3.3 shard_map.396
  334.2 17.7 %shard_map.397 = (f32[64,768]{1,0:T(8,128)}, f32[8,768]{1,0:T(8,128)}) custom-call(bf16[256,768]{1,0:T(8,128)(2,1)} %copy-done.23, f32[64,768]{1,0:T(8,128)} %get-tuple-element.91.refs_1_, f32[8,768]{1,0:T(8,128)} %copy-done.43), custom_call_target="tpu_custom_call" | custom-call | tf_op jit(solution)/shard_map/pallas_call | solution.py:281
  353.4 1.4 reshape.215
  354.8 3.0 fusion.66
  358.5 1.4 reshape.217
  359.9 3.2 fusion.67
  364.5 1.3 constant_dynamic-slice_fusion.2
  366.6 8.3 %all_to_all.50 = f32[8,1,128]{2,1,0:T(1,128)S(1)} all-to-all(f32[8,1,128]{2,1,0:T(1,128)S(1)} %bitcast.137), channel_id=1, replica_groups=mesh['dp'=8,'tensor'=4] {'dp'}, dimensions={0} | all-to-all | bytes 8192 | tf_op jit(solution)/shard_map/all_to_all | solution.py:502
  375.0 19.8 %all_to_all.51 = bf16[8,96,768]{2,1,0:T(8,128)(2,1)} all-to-all(bf16[8,96,768]{2,1,0:T(8,128)(2,1)S(1)} %bitcast.123), channel_id=1, replica_groups=mesh['dp'=8,'tensor'=4] {'dp'}, dimensions={0} | all-to-all | bytes 2359296 | tf_op jit(solution)/shard_map/all_to_all | solution.py:312
  394.8 3.7 all-to-all-start.6
  398.5 1.1 iota_compare_fusion.2
  399.6 15.6 %all-to-all-done.6 = bf16[8,96,768]{2,1,0:T(8,128)(2,1)S(1)} async-done(((bf16[8,96,768]{2,1,0:T(8,128)(2,1)}), bf16[8,96,768]{2,1,0:T(8,128)(2,1)S(1)}, u32[]{:S(2)}, u32[]{:S(2)}) %all-to-all-start.6) | async-done | bytes 1179680 | tf_op jit(solution)/shard_map/all_to_all | solution.py:312
  415.2 4.3 all-to-all-start.8
  419.5 5.4 %convolution_bitcast_fusion = f32[2,768,768]{2,1,0:T(8,128)} fusion(bf16[8,2,48,768]{3,2,0,1:T(8,128)(2,1)} %get-tuple-element.249, bf16[8,2,48,768]{3,2,1,0:T(8,128)(2,1)} %all-to-all-done), kind=kOutput, calls=%fused_computation.25 | convolution fusion | flops 905969664 | bytes 7077888 | tf_op jit(solution)/shard_map/secf,secd->efd/dot_general | solution.py:466
  424.9 3.6 convolution_bitcast_fusion.1
  428.6 2.9 multiply_reduce_fusion.refs_0_
  431.5 13.2 %shard_map.390 = f32[64,768]{1,0:T(8,128)} custom-call(bf16[256,768]{1,0:T(8,128)(2,1)} %multiply_reduce_fusion.refs_0_, f32[64,768]{1,0:T(8,128)} %get-tuple-element.74.refs_1_), custom_call_target="tpu_custom_call" | custom-call | tf_op jit(solution)/shard_map/pallas_call | solution.py:281
  445.3 4.2 all-to-all-start.7
  450.9 1.5 convert_reduce_fusion
  453.2 1.6 copy.182
  454.8 1.5 convert_reduce_fusion.3
  457.1 1.6 copy.181
  459.6 6.8 %all-to-all-done.7 = bf16[8,96,768]{2,1,0:T(8,128)(2,1)} async-done(((bf16[8,96,768]{2,1,0:T(8,128)(2,1)}), bf16[8,96,768]{2,1,0:T(8,128)(2,1)}, u32[]{:S(2)}, u32[]{:S(2)}) %all-to-all-start.7) | async-done | bytes 1179680 | tf_op jit(solution)/shard_map/all_to_all | solution.py:312
  466.3 2.2 convert_reduce_fusion.1
  (218 shorter events, 49.9 us)
Async XLA Ops:
  7.2 176.2 %copy-start = (bf16[2,768,768]{2,1,0:T(8,128)(2,1)S(1)}, bf16[2,768,768]{2,1,0:T(8,128)(2,1)}, u32[]{:S(2)}) copy-start(bf16[2,768,768]{2,1,0:T(8,128)(2,1)} %param.44) | copy-start | bytes 7077892
  7.2 5.6 %copy-start.54 = (bf16[96,192]{1,0:T(8,128)(2,1)S(1)}, bf16[96,192]{1,0:T(8,128)(2,1)}, u32[]{:S(2)}) copy-start(bf16[96,192]{1,0:T(8,128)(2,1)} %param.40) | copy-start | bytes 110596
  7.2 5.6 %copy-start.55 = (bf16[96,192]{1,0:T(8,128)(2,1)S(1)}, bf16[96,192]{1,0:T(8,128)(2,1)}, u32[]{:S(2)}) copy-start(bf16[96,192]{1,0:T(8,128)(2,1)} %param.39) | copy-start | bytes 110596
  7.2 5.6 %copy-start.56 = (bf16[96,192]{1,0:T(8,128)(2,1)S(1)}, bf16[96,192]{1,0:T(8,128)(2,1)}, u32[]{:S(2)}) copy-start(bf16[96,192]{1,0:T(8,128)(2,1)} %param.38) | copy-start | bytes 110596
  7.2 6.4 %copy-start.69 = (bf16[4,3]{1,0:T(4,128)(2,1)S(1)}, bf16[4,3]{1,0:T(4,128)(2,1)}, u32[]{:S(2)}) copy-start(bf16[4,3]{1,0:T(4,128)(2,1)} %param.33) | copy-start | bytes 76
  7.3 6.4 %copy-start.70 = (bf16[4,3]{1,0:T(4,128)(2,1)S(1)}, bf16[4,3]{1,0:T(4,128)(2,1)}, u32[]{:S(2)}) copy-start(bf16[4,3]{1,0:T(4,128)(2,1)} %param.42) | copy-start | bytes 76
  7.3 6.5 %copy-start.62 = (f32[256,2]{0,1:T(2,128)S(1)}, f32[256,2]{0,1:T(2,128)}, u32[]{:S(2)}) copy-start(f32[256,2]{0,1:T(2,128)} %param.27) | copy-start | bytes 6148
  7.3 6.5 %copy-start.61 = (s32[256,2]{0,1:T(2,128)S(1)}, s32[256,2]{0,1:T(2,128)}, u32[]{:S(2)}) copy-start(s32[256,2]{0,1:T(2,128)} %param.26) | copy-start | bytes 6148
  7.3 7.3 %copy-start.67 = (bf16[24]{0:T(256)(128)(2,1)S(1)}, bf16[24]{0:T(256)(128)(2,1)}, u32[]{:S(2)}) copy-start(bf16[24]{0:T(256)(128)(2,1)} %param.43) | copy-start | bytes 148
  7.3 7.3 %copy-start.66 = (bf16[24]{0:T(256)(128)(2,1)S(1)}, bf16[24]{0:T(256)(128)(2,1)}, u32[]{:S(2)}) copy-start(bf16[24]{0:T(256)(128)(2,1)} %param.37) | copy-start | bytes 148
  7.3 7.3 %copy-start.65 = (bf16[24]{0:T(256)(128)(2,1)S(1)}, bf16[24]{0:T(256)(128)(2,1)}, u32[]{:S(2)}) copy-start(bf16[24]{0:T(256)(128)(2,1)} %param.34) | copy-start | bytes 148
  7.3 7.3 %copy-start.64 = (bf16[24]{0:T(256)(128)(2,1)S(1)}, bf16[24]{0:T(256)(128)(2,1)}, u32[]{:S(2)}) copy-start(bf16[24]{0:T(256)(128)(2,1)} %param.28) | copy-start | bytes 148
  7.3 67.7 %all-gather.5.cloned.1.call-start = ((), (), s32[]{:S(2)}) async-start(), calls=%async_computation.9 | async-start | bytes 1327104 | tf_op jit(solution)/shard_map/all_gather | solution.py:388
  10.0 92.4 %all-gather.7.cloned.1.call-start = ((), (), s32[]{:S(2)}) async-start(), calls=%async_computation.10 | async-start | bytes 2654208 | tf_op jit(solution)/shard_map/all_gather | solution.py:388
  11.8 120.2 %all-gather.9.cloned.1.call-start = ((), (), s32[]{:S(2)}) async-start(), calls=%async_computation.11 | async-start | bytes 1327104 | tf_op jit(solution)/shard_map/all_gather | solution.py:388
  14.6 25.3 %copy-start.59 = (s32[1,2,2,128]{3,1,2,0:T(2,128)}, s32[1,2,2,128]{3,1,2,0:T(2,128)S(1)}, u32[]{:S(2)}) copy-start(s32[1,2,2,128]{3,1,2,0:T(2,128)S(1)} %copy.189) | copy-start | bytes 6148
  41.8 4.4 copy-start.41
  41.8 66.0 %all-to-all-start = ((bf16[8,2,48,768]{3,2,1,0:T(8,128)(2,1)}), bf16[8,2,48,768]{3,2,1,0:T(8,128)(2,1)}, u32[]{:S(2)}, u32[]{:S(2)}) async-start(bf16[8,2,48,768]{3,2,1,0:T(8,128)(2,1)} %bitcast.7), calls=%async_computation | async-start | bytes 2359296 | tf_op jit(solution)/shard_map/all_to_all | solution.py:317
  46.3 85.7 %copy-start.7 = (s32[256,1]{1,0:T(8,128)}, s32[256,1]{1,0:T(8,128)S(1)}, u32[]{:S(2)}) copy-start(s32[256,1]{1,0:T(8,128)S(1)} %copy.166.segc_ref) | copy-start | bytes 3076
  69.1 6.0 %copy-start.10 = (bf16[256,768]{1,0:T(8,128)(2,1)S(1)}, bf16[256,768]{1,0:T(8,128)(2,1)}, u32[]{:S(2)}) copy-start(bf16[256,768]{1,0:T(8,128)(2,1)} %get-tuple-element.62.x_ref) | copy-start | bytes 1179652
  72.3 59.8 %copy-start.35 = (f32[24,256]{1,0:T(8,128)}, f32[24,256]{1,0:T(8,128)S(1)}, u32[]{:S(2)}) copy-start(f32[24,256]{1,0:T(8,128)S(1)} %reshape.211.band_ref) | copy-start | bytes 73732
  74.2 31.9 %copy-start.33 = (f32[24,256]{1,0:T(8,128)}, f32[24,256]{1,0:T(8,128)S(1)}, u32[]{:S(2)}) copy-start(f32[24,256]{1,0:T(8,128)S(1)} %reshape.202.band_ref) | copy-start | bytes 73732
  74.4 141.9 %copy-start.57 = (f32[768]{0:T(1024)}, f32[768]{0:T(1024)S(1)}, u32[]{:S(2)}) copy-start(f32[768]{0:T(1024)S(1)} %reshape.231) | copy-start | bytes 9220
  75.1 1.3 copy-start.3
  102.5 1.7 copy-start.1
  104.2 1.0 copy-start.14
  132.1 1.3 copy-start.5
  133.4 1.0 copy-start.12
  162.5 53.8 %copy-start.58 = (f32[256]{0:T(256)}, f32[256]{0:T(256)S(1)}, u32[]{:S(2)}) copy-start(f32[256]{0:T(256)S(1)} %add_rsqrt_fusion) | copy-start | bytes 3076
  183.4 2.2 copy-start.49
  183.4 2.2 copy-start.68
  188.6 1.1 copy-start.71
  190.9 21.1 %all-to-all-start.3 = ((bf16[8,2,48,768]{3,2,1,0:T(8,128)(2,1)}), bf16[8,2,48,768]{3,2,1,0:T(8,128)(2,1)}, u32[]{:S(2)}, u32[]{:S(2)}) async-start(bf16[8,2,48,768]{3,2,1,0:T(8,128)(2,1)} %copy.174), calls=%async_computation.3 | async-start | bytes 2359296 | tf_op jit(solution)/shard_map/all_to_all | solution.py:317
  199.4 16.9 %copy-start.47 = (bf16[256,768]{1,0:T(8,128)(2,1)S(1)}, bf16[256,768]{1,0:T(8,128)(2,1)}, u32[]{:S(2)}) copy-start(bf16[256,768]{1,0:T(8,128)(2,1)} %get-tuple-element.73) | copy-start | bytes 1179652
  212.0 154.6 %all-to-all-start.2 = ((bf16[8,2,48,768]{3,2,1,0:T(8,128)(2,1)}), bf16[8,2,48,768]{3,2,1,0:T(8,128)(2,1)}, u32[]{:S(2)}, u32[]{:S(2)}) async-start(bf16[8,2,48,768]{3,2,1,0:T(8,128)(2,1)} %copy.172), calls=%async_computation.2 | async-start | bytes 2359296 | tf_op jit(solution)/shard_map/all_to_all | solution.py:317
  216.3 2.0 copy-start.48
  218.3 30.5 %copy-start.6 = (bf16[768,768]{1,0:T(8,128)(2,1)S(1)}, bf16[768,768]{1,0:T(8,128)(2,1)}, u32[]{:S(2)}) copy-start(bf16[768,768]{1,0:T(8,128)(2,1)} %all-gather.9.cloned.1.call-done.w_ref) | copy-start | bytes 3538948
  248.7 0.9 copy-start.8
  249.6 1.0 copy-start.13
  250.6 1.0 copy-start.21
  251.6 1.0 copy-start.32
  253.3 0.9 copy-start.40
  287.4 1.7 copy-start.2
  289.0 1.0 copy-start.15
  290.0 1.1 copy-start.19
  291.2 1.0 copy-start.28
  292.2 30.2 %copy-start.4 = (bf16[768,768]{1,0:T(8,128)(2,1)S(1)}, bf16[768,768]{1,0:T(8,128)(2,1)}, u32[]{:S(2)}) copy-start(bf16[768,768]{1,0:T(8,128)(2,1)} %all-gather.5.cloned.1.call-done.w_ref) | copy-start | bytes 3538948
  322.3 0.9 copy-start.9
  323.3 1.0 copy-start.11
  324.2 1.0 copy-start.20
  325.2 1.0 copy-start.30
  327.0 0.9 copy-start.38
  331.2 1.1 copy-start.16
  334.2 40.7 %copy-start.17 = (bf16[768,768]{1,0:T(8,128)(2,1)S(1)}, bf16[768,768]{1,0:T(8,128)(2,1)}, u32[]{:S(2)}) copy-start(bf16[768,768]{1,0:T(8,128)(2,1)} %copy-done.16) | copy-start | bytes 3538948
  394.8 3.7 copy-start.60
  394.8 20.4 %all-to-all-start.6 = ((bf16[8,96,768]{2,1,0:T(8,128)(2,1)}), bf16[8,96,768]{2,1,0:T(8,128)(2,1)S(1)}, u32[]{:S(2)}, u32[]{:S(2)}) async-start(bf16[8,96,768]{2,1,0:T(8,128)(2,1)} %bitcast.30), calls=%async_computation.6 | async-start | bytes 2359296 | tf_op jit(solution)/shard_map/all_to_all | solution.py:312
  415.2 30.0 %all-to-all-start.8 = ((bf16[8,96,768]{2,1,0:T(8,128)(2,1)}), bf16[8,96,768]{2,1,0:T(8,128)(2,1)}, u32[]{:S(2)}, u32[]{:S(2)}) async-start(bf16[8,96,768]{2,1,0:T(8,128)(2,1)} %bitcast.33), calls=%async_computation.8 | async-start | bytes 2359296 | tf_op jit(solution)/shard_map/all_to_all | solution.py:312
  419.5 5.4 %copy-start.50 = (bf16[8,2,48,768]{3,2,1,0:T(8,128)(2,1)S(1)}, bf16[8,2,48,768]{3,2,1,0:T(8,128)(2,1)}, u32[]{:S(2)}) copy-start(bf16[8,2,48,768]{3,2,1,0:T(8,128)(2,1)} %copy-done.49) | copy-start | bytes 3538948
  419.5 5.4 %copy-start.72 = (bf16[8,2,48,768]{3,2,0,1:T(8,128)(2,1)S(1)}, bf16[8,2,48,768]{3,2,0,1:T(8,128)(2,1)}, u32[]{:S(2)}) copy-start(bf16[8,2,48,768]{3,2,0,1:T(8,128)(2,1)} %copy-done.71) | copy-start | bytes 3538948
  424.9 3.7 copy-start.52
  424.9 3.7 copy-start.63
  445.3 21.1 %all-to-all-start.7 = ((bf16[8,96,768]{2,1,0:T(8,128)(2,1)}), bf16[8,96,768]{2,1,0:T(8,128)(2,1)}, u32[]{:S(2)}, u32[]{:S(2)}) async-start(bf16[8,96,768]{2,1,0:T(8,128)(2,1)} %bitcast.31), calls=%async_computation.7 | async-start | bytes 2359296 | tf_op jit(solution)/shard_map/all_to_all | solution.py:312
  459.6 8.9 %copy-start.51 = (f32[64,768]{1,0:T(8,128)S(1)}, f32[64,768]{1,0:T(8,128)}, u32[]{:S(2)}) copy-start(f32[64,768]{1,0:T(8,128)} %shard_map.390) | copy-start | bytes 589828
  459.6 9.6 %copy-start.53 = (f32[64,768]{1,0:T(8,128)S(1)}, f32[64,768]{1,0:T(8,128)}, u32[]{:S(2)}) copy-start(f32[64,768]{1,0:T(8,128)} %get-tuple-element.276) | copy-start | bytes 589828
  (18 other events, 12.7 us)
Sparse Core Ops, SparseCore 0:
  10.6 26.6 all-gather.4
  39.7 38.3 all-gather.6
  80.5 23.9 all-gather.8
